TPU v7x, 32 devices: a whole 2x2x4 slice. The times are simulated.
32 devices in a mesh: dp: 4 (over z), expert: 8 (over y, x, core).
Axes of the slice: x: 2, y: 2, z: 4, core: 2. Of those that a mesh axis runs over, the one named last changes fastest.
Arguments:
- tokens: bfloat16 [4096, 2048], P(('dp', 'expert')), may hold values from -6 to 6
- routes: int32 [4096, 8], P(('dp', 'expert')), may hold values from 0 to 31, all different within a row; in each aligned block of 128 rows (0 to 127, 128 to 255, ...) at most 38 rows name the same one
- prefix_len: int32 [4], P('dp'), may hold values from 102 to 512
- query_weight: bfloat16 [2048, 4096], P('dp', 'expert'), may hold values from -0.125 to 0.125
- key_matrix: bfloat16 [2048, 512], P('dp', 'expert'), may hold values from -0.125 to 0.125
- value_matrix: bfloat16 [2048, 512], P('dp', 'expert'), may hold values from -0.125 to 0.125
- out_weight: bfloat16 [4096, 2048], P('dp', 'expert'), may hold values from -2 to 2
- router_weight: bfloat16 [2048, 32], P('dp', 'expert'), may hold values from -0.0625 to 0.0625
- attention_gain: float32 [2048], replicated, may hold values from 0.25 to 1.75
- mixture_gain: float32 [2048], replicated, may hold values from 0.25 to 1.75
- query_gain: float32 [128], replicated, may hold values from 0.25 to 1.75
- key_norm_gain: float32 [128], replicated, may hold values from 0.25 to 1.75
- expert_gate: bfloat16 [32, 2048, 768], P(('dp', 'expert')), may hold values from -0.125 to 0.125
- expert_up: bfloat16 [32, 2048, 768], P(('dp', 'expert')), may hold values from -0.125 to 0.125
- expert_down: bfloat16 [32, 768, 2048], P(('dp', 'expert')), may hold values from -0.875 to 0.875
- cotangent: bfloat16 [4096, 2048], P(('dp', 'expert')), may hold values from -6 to 6
Outputs:
- layer_out: bfloat16 [4096, 2048], P(('dp', 'expert'))
- input_grad: float32 [4096, 2048], P(('dp', 'expert'))
- query_weight_grad: float32 [2048, 4096], P('dp', 'expert')
- key_weight_grad: float32 [2048, 512], P('dp', 'expert')
- value_weight_grad: float32 [2048, 512], P('dp', 'expert')
- out_weight_grad: float32 [4096, 2048], P('dp', 'expert')
- router_grad: float32 [2048, 32], P('dp', 'expert')
- attention_gain_grad: float32 [2048], replicated
- mixture_gain_grad: float32 [2048], replicated
- query_gain_grad: float32 [128], replicated
- key_gain_grad: float32 [128], replicated
- expert_gate_grad: float32 [32, 2048, 768], P(('dp', 'expert'))
- expert_up_grad: float32 [32, 2048, 768], P(('dp', 'expert'))
- expert_down_grad: float32 [32, 768, 2048], P(('dp', 'expert'))
Inputs may be any that keep to these rules, and one draw needn't show every extreme that they name: `routes`: each row names 8 different experts. In the rows of one device no expert is named more than 38 times, and in every draw the rows of some device name some expert exactly 38 times.
All inputs are finite; a program needn't handle non-finite values.
Results may differ from a plain program's by a relative error of at most 0.025.
Values may be sent and summed in bfloat16 or wider, within the bound.
No kernel may reach another device: no remote copies, remote signals or barrier semaphores. Data moves between devices by JAX's collectives and lax.ppermute only.
A program may use at most 256 MiB of HBM per device.

v0:
```python
import math

import jax
import jax.numpy as jnp
from jax import lax
from jax.sharding import PartitionSpec as P

MODEL_WIDTH = 2048
QUERY_HEADS = 32
KEY_VALUE_HEADS = 4
HEAD_SIZE = 128
TOP = 8
EXP_DEV = 1


EPS = 1e-06
ROTARY_BASE = 1000000.0
VERY_NEGATIVE = -1e30


def head_normalize(source, gain_row):
    scaling = lax.rsqrt(jnp.mean(source * source, axis=-1, keepdims=True) + EPS)
    return (source * scaling * gain_row, scaling)


def normalize_back(upstream, source, scaling, gain_row):
    unit_rows = source * scaling
    weighted = upstream * gain_row
    inner_mean = jnp.mean(weighted * unit_rows, axis=-1, keepdims=True)
    return (scaling * (weighted - unit_rows * inner_mean), upstream * unit_rows)


def rotary(offset, span_length):
    half_dim = HEAD_SIZE // 2
    frequency = jnp.power(ROTARY_BASE, -jnp.arange(half_dim, dtype=jnp.float32) * 2.0 / HEAD_SIZE)
    places = (offset + jnp.arange(span_length, dtype=jnp.int32)).astype(jnp.float32)
    angles = places[:, None] * frequency[None, :]
    cosine_lookup = jnp.concatenate([jnp.cos(angles), jnp.cos(angles)], axis=-1)[:, None, :]
    sine_lookup = jnp.concatenate([jnp.sin(angles), jnp.sin(angles)], axis=-1)[:, None, :]
    return (cosine_lookup, sine_lookup)


def rotary_apply(source, cosine_lookup, sine_lookup):
    half_dim = source.shape[-1] // 2
    front_half = source[..., :half_dim]
    back_half = source[..., half_dim:]
    return source * cosine_lookup + jnp.concatenate([-back_half, front_half], axis=-1) * sine_lookup


def rotate_back(upstream, cosine_lookup, sine_lookup):
    half_dim = upstream.shape[-1] // 2
    turned = upstream * sine_lookup
    return upstream * cosine_lookup + jnp.concatenate(
        [turned[..., half_dim:], -turned[..., :half_dim]], axis=-1
    )


def shards(
    tokens,
    routes,
    prefix_len,
    query_weight,
    key_matrix,
    value_matrix,
    out_weight,
    router_weight,
    attention_gain,
    mixture_gain,
    query_gain,
    key_norm_gain,
    expert_gate,
    expert_up,
    expert_down,
    cotangent,
):
    resident_tokens = tokens.shape[0]
    head_groups = QUERY_HEADS // KEY_VALUE_HEADS
    softmax_scale = HEAD_SIZE ** (-0.5)
    query_rows, key_rows, value_rows, out_rows, router_rows = (
        lax.all_gather(query_weight, "dp", axis=0, tiled=True),
        lax.all_gather(key_matrix, "dp", axis=0, tiled=True),
        lax.all_gather(value_matrix, "dp", axis=0, tiled=True),
        lax.all_gather(out_weight, "dp", axis=0, tiled=True),
        lax.all_gather(router_weight, "dp", axis=0, tiled=True),
    )
    query_full, key_full, value_full, out_full, router_full = (
        lax.all_gather(query_rows, "expert", axis=1, tiled=True),
        lax.all_gather(key_rows, "expert", axis=1, tiled=True),
        lax.all_gather(value_rows, "expert", axis=1, tiled=True),
        lax.all_gather(out_rows, "expert", axis=1, tiled=True),
        lax.all_gather(router_rows, "expert", axis=1, tiled=True),
    )
    experts_all = router_full.shape[1]
    dp_count = lax.axis_size("dp")
    expert_count = lax.axis_size("expert")
    devices = dp_count * expert_count
    capacity = max(2, 6 * resident_tokens * TOP // (5 * experts_all))
    residual_in = tokens.astype(jnp.float32)
    normed, scale_attention = head_normalize(residual_in, attention_gain)
    normed_low = normed.astype(jnp.bfloat16)
    query_raw = jnp.dot(normed_low, query_full, preferred_element_type=jnp.float32).reshape(
        resident_tokens, QUERY_HEADS, HEAD_SIZE
    )
    key_unnormed = jnp.dot(normed_low, key_full, preferred_element_type=jnp.float32).reshape(
        resident_tokens, KEY_VALUE_HEADS, HEAD_SIZE
    )
    value_raw = jnp.dot(normed_low, value_full, preferred_element_type=jnp.float32).reshape(
        resident_tokens, KEY_VALUE_HEADS, HEAD_SIZE
    )
    offset = lax.axis_index("expert") * resident_tokens
    cosine_lookup, sine_lookup = rotary(offset, resident_tokens)
    query_normed, scale_query = head_normalize(query_raw, query_gain)
    query_narrow = (
        rotary_apply(query_normed, cosine_lookup, sine_lookup)
        .astype(jnp.bfloat16)
        .reshape(resident_tokens, KEY_VALUE_HEADS, head_groups, HEAD_SIZE)
    )
    key_normed, scale_key = head_normalize(key_unnormed, key_norm_gain)
    key_low = rotary_apply(key_normed, cosine_lookup, sine_lookup).astype(jnp.bfloat16)
    value_narrow = value_raw.astype(jnp.bfloat16)
    every_key, every_value = (
        lax.all_gather(key_low, "expert", axis=0, tiled=True),
        lax.all_gather(value_narrow, "expert", axis=0, tiled=True),
    )
    span_length = every_key.shape[0]
    segment_rows = math.gcd(span_length, 768)
    segment_list = span_length // segment_rows
    key_segments = every_key.reshape(segment_list, segment_rows, KEY_VALUE_HEADS, HEAD_SIZE)
    value_segments = every_value.reshape(segment_list, segment_rows, KEY_VALUE_HEADS, HEAD_SIZE)
    piece_starts = jnp.arange(segment_list, dtype=jnp.int32) * segment_rows
    query_place = offset + jnp.arange(resident_tokens, dtype=jnp.int32)
    prefix = prefix_len[0]

    def scores_of(key_piece, piece_start):
        raw_scores = (
            jnp.einsum(
                "thgd,shd->hgts", query_narrow, key_piece, preferred_element_type=jnp.float32
            )
            * softmax_scale
        )
        key_place = piece_start + jnp.arange(segment_rows, dtype=jnp.int32)
        allowed = (key_place[None, :] <= query_place[:, None]) | (key_place[None, :] < prefix)
        return (raw_scores, allowed)

    def running_stats(running, inputs):
        highest, totals = running
        key_piece, piece_start = inputs
        raw_scores, allowed = scores_of(key_piece, piece_start)
        new_high = jnp.maximum(
            highest, jnp.max(jnp.where(allowed, raw_scores, VERY_NEGATIVE), axis=-1)
        )
        weights_now = jnp.where(allowed, jnp.exp(raw_scores - new_high[..., None]), 0.0)
        totals = totals * jnp.exp(highest - new_high) + jnp.sum(weights_now, axis=-1)
        return ((new_high, totals), None)

    initial_maximum = jnp.full(
        (KEY_VALUE_HEADS, head_groups, resident_tokens), VERY_NEGATIVE, jnp.float32
    )
    initial_sums = jnp.zeros((KEY_VALUE_HEADS, head_groups, resident_tokens), jnp.float32)
    (highest, totals), _ = lax.scan(
        running_stats, (initial_maximum, initial_sums), (key_segments, piece_starts)
    )
    log_total = highest + jnp.log(totals)

    def probabilities(key_piece, piece_start):
        raw_scores, allowed = scores_of(key_piece, piece_start)
        return jnp.where(allowed, jnp.exp(raw_scores - log_total[..., None]), 0.0)

    def attend_piece(accumulated, inputs):
        key_piece, value_piece, piece_start = inputs
        weights_low = probabilities(key_piece, piece_start).astype(jnp.bfloat16)
        accumulated = accumulated + jnp.einsum(
            "hgts,shd->thgd", weights_low, value_piece, preferred_element_type=jnp.float32
        )
        return (accumulated, None)

    attended, _ = lax.scan(
        attend_piece,
        jnp.zeros((resident_tokens, KEY_VALUE_HEADS, head_groups, HEAD_SIZE), jnp.float32),
        (key_segments, value_segments, piece_starts),
    )
    attended_low = attended.reshape(resident_tokens, QUERY_HEADS * HEAD_SIZE).astype(jnp.bfloat16)
    after_attn = residual_in + jnp.dot(attended_low, out_full, preferred_element_type=jnp.float32)
    mixed_in, scale_mixture = head_normalize(after_attn, mixture_gain)
    mixed_low = mixed_in.astype(jnp.bfloat16)
    logits = jnp.dot(mixed_low, router_full, preferred_element_type=jnp.float32)
    expert_ids = jnp.arange(experts_all, dtype=jnp.int32)
    chosen_mask = (routes[:, :, None] == expert_ids[None, None, :]).astype(jnp.float32)
    chosen = jnp.sum(chosen_mask * logits[:, None, :], axis=-1)
    route_weight = jax.nn.softmax(chosen, axis=-1)
    flat_routes = routes.reshape(-1)
    flat_hot = (flat_routes[:, None] == expert_ids[None, :]).astype(jnp.int32)
    slot_rank = jnp.sum(jnp.cumsum(flat_hot, axis=0) * flat_hot, axis=1) - 1
    slot_index = flat_routes * capacity + slot_rank
    outgoing = (
        jnp.zeros((experts_all * capacity, MODEL_WIDTH), jnp.bfloat16)
        .at[slot_index]
        .set(jnp.repeat(mixed_low, TOP, axis=0))
    )
    arrived = lax.all_to_all(
        outgoing.reshape(devices, EXP_DEV * capacity, MODEL_WIDTH),
        ("dp", "expert"),
        split_axis=0,
        concat_axis=0,
        tiled=True,
    )
    arrived = arrived.reshape(devices, EXP_DEV, capacity, MODEL_WIDTH)
    gate_raw = jnp.einsum(
        "necd,edf->necf", arrived, expert_gate, preferred_element_type=jnp.float32
    )
    up_raw = jnp.einsum("necd,edf->necf", arrived, expert_up, preferred_element_type=jnp.float32)
    gate_sig = jax.nn.sigmoid(gate_raw)
    activated = (gate_raw * gate_sig * up_raw).astype(jnp.bfloat16)
    produced = jnp.einsum(
        "necf,efd->necd", activated, expert_down, preferred_element_type=jnp.float32
    ).astype(jnp.bfloat16)
    returned = lax.all_to_all(
        produced.reshape(devices, EXP_DEV * capacity, MODEL_WIDTH),
        ("dp", "expert"),
        split_axis=0,
        concat_axis=0,
        tiled=True,
    )
    picked = (
        returned.reshape(experts_all * capacity, MODEL_WIDTH)[slot_index]
        .reshape(resident_tokens, TOP, MODEL_WIDTH)
        .astype(jnp.float32)
    )
    mixture = jnp.sum(picked * route_weight[:, :, None], axis=1)
    layer_out = (after_attn + mixture).astype(jnp.bfloat16)
    upstream = cotangent.astype(jnp.float32)
    route_grad = jnp.sum(picked * upstream[:, None, :], axis=-1)
    chosen_grad = route_weight * (
        route_grad - jnp.sum(route_weight * route_grad, axis=-1, keepdims=True)
    )
    logit_grad = jnp.sum(chosen_mask * chosen_grad[:, :, None], axis=1).astype(jnp.bfloat16)
    mixed_grad = jnp.dot(logit_grad, router_full.T, preferred_element_type=jnp.float32)
    produced_grad = (
        (route_weight[:, :, None] * upstream[:, None, :])
        .astype(jnp.bfloat16)
        .reshape(resident_tokens * TOP, MODEL_WIDTH)
    )
    outgoing_grad = (
        jnp.zeros((experts_all * capacity, MODEL_WIDTH), jnp.bfloat16)
        .at[slot_index]
        .set(produced_grad)
    )
    arrived_grad = lax.all_to_all(
        outgoing_grad.reshape(devices, EXP_DEV * capacity, MODEL_WIDTH),
        ("dp", "expert"),
        split_axis=0,
        concat_axis=0,
        tiled=True,
    )
    arrived_grad = arrived_grad.reshape(devices, EXP_DEV, capacity, MODEL_WIDTH)
    down_gradient = jnp.einsum(
        "necf,necd->efd", activated, arrived_grad, preferred_element_type=jnp.float32
    )
    activated_grad = jnp.einsum(
        "necd,efd->necf", arrived_grad, expert_down, preferred_element_type=jnp.float32
    )
    gate_grad = (activated_grad * up_raw * gate_sig * (1.0 + gate_raw * (1.0 - gate_sig))).astype(
        jnp.bfloat16
    )
    up_grad = (activated_grad * gate_raw * gate_sig).astype(jnp.bfloat16)
    gate_gradient = jnp.einsum(
        "necd,necf->edf", arrived, gate_grad, preferred_element_type=jnp.float32
    )
    up_gradient = jnp.einsum("necd,necf->edf", arrived, up_grad, preferred_element_type=jnp.float32)
    row_grad = (
        jnp.einsum("necf,edf->necd", gate_grad, expert_gate, preferred_element_type=jnp.float32)
        + jnp.einsum("necf,edf->necd", up_grad, expert_up, preferred_element_type=jnp.float32)
    ).astype(jnp.bfloat16)
    back_rows = lax.all_to_all(
        row_grad.reshape(devices, EXP_DEV * capacity, MODEL_WIDTH),
        ("dp", "expert"),
        split_axis=0,
        concat_axis=0,
        tiled=True,
    )
    back_picked = back_rows.reshape(experts_all * capacity, MODEL_WIDTH)[slot_index].reshape(
        resident_tokens, TOP, MODEL_WIDTH
    )
    mixed_grad = mixed_grad + jnp.sum(back_picked.astype(jnp.float32), axis=1)
    mixture_back, mixture_terms = normalize_back(
        mixed_grad, after_attn, scale_mixture, mixture_gain
    )
    after_grad = upstream + mixture_back
    after_low = after_grad.astype(jnp.bfloat16)
    attended_gradient = jnp.dot(after_low, out_full.T, preferred_element_type=jnp.float32).astype(
        jnp.bfloat16
    )
    attended_gradient = attended_gradient.reshape(
        resident_tokens, KEY_VALUE_HEADS, head_groups, HEAD_SIZE
    )

    def delta_piece(row_delta, inputs):
        key_piece, value_piece, piece_start = inputs
        weights_full = probabilities(key_piece, piece_start)
        prob_grad = jnp.einsum(
            "thgd,shd->hgts", attended_gradient, value_piece, preferred_element_type=jnp.float32
        )
        return (row_delta + jnp.sum(weights_full * prob_grad, axis=-1), None)

    row_delta, _ = lax.scan(
        delta_piece,
        jnp.zeros((KEY_VALUE_HEADS, head_groups, resident_tokens), jnp.float32),
        (key_segments, value_segments, piece_starts),
    )

    def backward_piece(query_sum, inputs):
        key_piece, value_piece, piece_start = inputs
        weights_full = probabilities(key_piece, piece_start)
        weights_low = weights_full.astype(jnp.bfloat16)
        prob_grad = jnp.einsum(
            "thgd,shd->hgts", attended_gradient, value_piece, preferred_element_type=jnp.float32
        )
        score_grad = (weights_full * (prob_grad - row_delta[..., None])).astype(jnp.bfloat16)
        query_sum = query_sum + jnp.einsum(
            "hgts,shd->thgd", score_grad, key_piece, preferred_element_type=jnp.float32
        )
        key_part = (
            jnp.einsum(
                "hgts,thgd->shd", score_grad, query_narrow, preferred_element_type=jnp.float32
            )
            * softmax_scale
        )
        value_part = jnp.einsum(
            "hgts,thgd->shd", weights_low, attended_gradient, preferred_element_type=jnp.float32
        )
        return (query_sum, (key_part, value_part))

    query_sum, (key_portions, value_portions) = lax.scan(
        backward_piece,
        jnp.zeros((resident_tokens, KEY_VALUE_HEADS, head_groups, HEAD_SIZE), jnp.float32),
        (key_segments, value_segments, piece_starts),
    )
    key_grad, value_gradient_full = (
        lax.psum_scatter(
            key_portions.reshape(span_length, KEY_VALUE_HEADS, HEAD_SIZE).astype(jnp.bfloat16),
            "expert",
            scatter_dimension=0,
            tiled=True,
        ).astype(jnp.float32),
        lax.psum_scatter(
            value_portions.reshape(span_length, KEY_VALUE_HEADS, HEAD_SIZE).astype(jnp.bfloat16),
            "expert",
            scatter_dimension=0,
            tiled=True,
        ).astype(jnp.float32),
    )
    query_turn = rotate_back(
        (query_sum * softmax_scale).reshape(resident_tokens, QUERY_HEADS, HEAD_SIZE),
        cosine_lookup,
        sine_lookup,
    )
    query_back, query_terms = normalize_back(query_turn, query_raw, scale_query, query_gain)
    key_turn = rotate_back(key_grad, cosine_lookup, sine_lookup)
    key_reverse, key_terms = normalize_back(key_turn, key_unnormed, scale_key, key_norm_gain)
    query_grad_low = query_back.reshape(resident_tokens, QUERY_HEADS * HEAD_SIZE).astype(
        jnp.bfloat16
    )
    key_gradient_narrow = key_reverse.reshape(resident_tokens, KEY_VALUE_HEADS * HEAD_SIZE).astype(
        jnp.bfloat16
    )
    value_gradient_narrow = value_gradient_full.reshape(
        resident_tokens, KEY_VALUE_HEADS * HEAD_SIZE
    ).astype(jnp.bfloat16)
    normed_grad = (
        jnp.dot(query_grad_low, query_full.T, preferred_element_type=jnp.float32)
        + jnp.dot(key_gradient_narrow, key_full.T, preferred_element_type=jnp.float32)
        + jnp.dot(value_gradient_narrow, value_full.T, preferred_element_type=jnp.float32)
    )
    input_back, attention_terms = normalize_back(
        normed_grad, residual_in, scale_attention, attention_gain
    )
    input_grad = after_grad + input_back
    attention_total, mixture_total, query_total, key_total = lax.psum(
        (
            jnp.sum(attention_terms, axis=0),
            jnp.sum(mixture_terms, axis=0),
            jnp.sum(query_terms, axis=(0, 1)),
            jnp.sum(key_terms, axis=(0, 1)),
        ),
        ("dp", "expert"),
    )
    query_gradient = jnp.dot(normed_low.T, query_grad_low, preferred_element_type=jnp.float32)
    key_gradient = jnp.dot(normed_low.T, key_gradient_narrow, preferred_element_type=jnp.float32)
    value_gradient = jnp.dot(
        normed_low.T, value_gradient_narrow, preferred_element_type=jnp.float32
    )
    out_gradient = jnp.dot(attended_low.T, after_low, preferred_element_type=jnp.float32)
    router_gradient = jnp.dot(mixed_low.T, logit_grad, preferred_element_type=jnp.float32)
    query_share, key_share, value_share, out_share, router_share = (
        lax.psum_scatter(
            query_gradient.astype(jnp.bfloat16), "expert", scatter_dimension=1, tiled=True
        ).astype(jnp.float32),
        lax.psum_scatter(
            key_gradient.astype(jnp.bfloat16), "expert", scatter_dimension=1, tiled=True
        ).astype(jnp.float32),
        lax.psum_scatter(
            value_gradient.astype(jnp.bfloat16), "expert", scatter_dimension=1, tiled=True
        ).astype(jnp.float32),
        lax.psum_scatter(
            out_gradient.astype(jnp.bfloat16), "expert", scatter_dimension=1, tiled=True
        ).astype(jnp.float32),
        lax.psum_scatter(
            router_gradient.astype(jnp.bfloat16), "expert", scatter_dimension=1, tiled=True
        ).astype(jnp.float32),
    )
    query_share, key_share, value_share, out_share, router_share = (
        lax.psum_scatter(
            query_share.astype(jnp.bfloat16), "dp", scatter_dimension=0, tiled=True
        ).astype(jnp.float32),
        lax.psum_scatter(
            key_share.astype(jnp.bfloat16), "dp", scatter_dimension=0, tiled=True
        ).astype(jnp.float32),
        lax.psum_scatter(
            value_share.astype(jnp.bfloat16), "dp", scatter_dimension=0, tiled=True
        ).astype(jnp.float32),
        lax.psum_scatter(
            out_share.astype(jnp.bfloat16), "dp", scatter_dimension=0, tiled=True
        ).astype(jnp.float32),
        lax.psum_scatter(
            router_share.astype(jnp.bfloat16), "dp", scatter_dimension=0, tiled=True
        ).astype(jnp.float32),
    )
    return (
        layer_out,
        input_grad,
        query_share,
        key_share,
        value_share,
        out_share,
        router_share,
        attention_total,
        mixture_total,
        query_total,
        key_total,
        gate_gradient,
        up_gradient,
        down_gradient,
    )


def solution(mesh):
    in_specs = (
        P(("dp", "expert"), None),
        P(("dp", "expert"), None),
        P("dp"),
        P("dp", "expert"),
        P("dp", "expert"),
        P("dp", "expert"),
        P("dp", "expert"),
        P("dp", "expert"),
        P(),
        P(),
        P(),
        P(),
        P(("dp", "expert"), None, None),
        P(("dp", "expert"), None, None),
        P(("dp", "expert"), None, None),
        P(("dp", "expert"), None),
    )
    out_specs = (
        P(("dp", "expert"), None),
        P(("dp", "expert"), None),
        P("dp", "expert"),
        P("dp", "expert"),
        P("dp", "expert"),
        P("dp", "expert"),
        P("dp", "expert"),
        P(),
        P(),
        P(),
        P(),
        P(("dp", "expert"), None, None),
        P(("dp", "expert"), None, None),
        P(("dp", "expert"), None, None),
    )
    return jax.shard_map(shards, mesh=mesh, in_specs=in_specs, out_specs=out_specs, check_vma=False)
```

profile of v0, /device:TPU:0, one launch (start us, length us, event | category | flops | bytes accessed | tf_op | source)
XLA Modules:
  0.0 1740.7 jit_solution(12718168279034576137)
XLA Ops:
  7.2 17.7 %all_gather.39 = bf16[2048,64]{0,1:T(8,128)(2,1)} all-gather(bf16[512,64]{0,1:T(8,128)(2,1)} %param.28), channel_id=1, replica_groups=mesh['dp'=4,'expert'=8] {'dp'}, dimensions={0}, use_global_device_ids=true | all-gather | bytes 327680 | tf_op jit(solution)/shard_map/all_gather | solution.py:81
  25.8 14.9 all_gather.36
  43.8 9.0 all-gather.14.cloned.1.call-done
  61.6 38.6 %all-gather.18.cloned.1.call-done = bf16[2048,512]{1,0:T(8,128)(2,1)} async-done(((bf16[512,512]{1,0:T(8,128)(2,1)}), bf16[2048,512]{1,0:T(8,128)(2,1)}) %all-gather.18.cloned.1.call-update) | async-done | bytes 2097168 | tf_op jit(solution)/shard_map/all_gather | solution.py:80
  100.2 28.4 %all-gather.10.cloned.1.call-done = bf16[2048,512]{0,1:T(8,128)(2,1)} async-done(((bf16[2048,64]{0,1:T(8,128)(2,1)}), bf16[2048,512]{0,1:T(8,128)(2,1)}) %all-gather.10.cloned.1.call-update) | async-done | bytes 2097168 | tf_op jit(solution)/shard_map/all_gather | solution.py:89
  132.2 43.5 %all-gather.22.cloned.1.call-done = bf16[4096,256]{1,0:T(8,128)(2,1)} async-done(((bf16[1024,256]{1,0:T(8,128)(2,1)}), bf16[4096,256]{1,0:T(8,128)(2,1)}) %all-gather.22.cloned.1.call-update) | async-done | bytes 2097168 | tf_op jit(solution)/shard_map/all_gather | solution.py:83
  177.0 9.0 reduce-window.6
  187.2 13.1 all-gather.16.cloned.1.call-done
  202.6 92.5 %all-gather.20.cloned.1.call-done = bf16[2048,4096]{1,0:T(8,128)(2,1)} async-done(((bf16[2048,512]{1,0:T(8,128)(2,1)}), bf16[2048,4096]{1,0:T(8,128)(2,1)}) %all-gather.20.cloned.1.call-update) | async-done | bytes 16777232 | tf_op jit(solution)/shard_map/all_gather | solution.py:87
  295.1 9.7 fusion.147
  315.8 39.9 %while.50 = (s32[]{:T(128)}, f32[4,8,128]{2,1,0:T(8,128)S(1)}, f32[4,8,128]{2,1,0:T(8,128)S(1)}, s32[4]{0:T(128)S(1)}, s32[]{:T(128)}, /*index=5*/bf16[4,256,4,1...) while((s32[]{:T(128)}, f32[4,8,128]{2,1,0:T(8,128)S(1)}, ...), condition=%wide.region_6.7_spmd.clone, body=%wide.region_3.6_spmd.clone.sunk | while | flops 275862400 | bytes 10014860 | solution.py:160
  318.5 4.1 fusion.227
  328.4 4.3 fusion.227
  338.7 4.1 fusion.227
  355.8 28.8 %while.51 = (s32[]{:T(128)}, f32[128,4,8,128]{0,3,2,1:T(8,128)}, bf16[4,256,4,128]{3,1,0,2:T(8,128)(2,1)}, s32[4]{0:T(128)S(1)}, s32[]{:T(128)}, /*index=5*/bf16...) while((s32[]{:T(128)}, f32[128,4,8,128]{0,3,2,1:T(8,128)}, ...), condition=%wide.region_8.9_spmd.clone, body=%wide.region_7.8_spmd.clone.sunk | while | flops 542180224 | bytes 5853843 | solution.py:177
  365.1 4.8 bitcast_add_fusion.5
  372.6 4.7 bitcast_add_fusion.5
  380.0 4.6 bitcast_add_fusion.5
  387.3 28.6 %all-gather.24.cloned.1.call-done = bf16[4096,2048]{1,0:T(8,128)(2,1)} async-done(((bf16[4096,256]{1,0:T(8,128)(2,1)}), bf16[4096,2048]{1,0:T(8,128)(2,1)}) %all-gather.24.cloned.1.call-update) | async-done | bytes 16777232 | tf_op jit(solution)/shard_map/all_gather | solution.py:90
  415.9 8.6 multiply_reduce_fusion.5
  426.4 10.4 scatter_custom_fusion
  436.8 7.4 reshape.444
  444.2 4.7 all-to-all-start
  449.0 122.0 %all_gather.46 = bf16[2048,4]{0,1:T(4,128)(2,1)S(1)} all-gather(bf16[512,4]{0,1:T(4,128)(2,1)S(1)} %copy-done.48), channel_id=1, replica_groups=mesh['dp'=4,'expert'=8] {'dp'}, dimensions={0}, use_global_device_ids=true | all-gather | bytes 20480 | tf_op jit(solution)/shard_map/all_gather | solution.py:84
  571.0 8.7 all-gather
  583.4 10.5 scatter_custom_fusion.1
  593.9 7.5 reshape.450
  601.4 4.2 all-to-all-start.2
  605.6 9.8 fusion.100
  615.4 8.7 fusion.96
  624.1 97.9 %all-to-all-done.2 = bf16[32,38,2048]{2,1,0:T(8,128)(2,1)} async-done(((bf16[32,38,2048]{2,1,0:T(8,128)(2,1)}), bf16[32,38,2048]{2,1,0:T(8,128)(2,1)}, u32[]{:S(2)}, u32[]{:S(2)}) %all-to-all-start.2) | async-done | bytes 4980768 | tf_op jit(solution)/shard_map/all_to_all | solution.py:248
  722.0 10.8 fusion.86
  734.2 6.0 convolution_convert_fusion.3
  744.1 6.0 fusion.98
  750.2 7.9 add_convert_fusion
  758.0 102.5 %all-to-all-done.1 = bf16[32,38,2048]{2,1,0:T(8,128)(2,1)} async-done(((bf16[32,38,2048]{2,1,0:T(8,128)(2,1)}), bf16[32,38,2048]{2,1,0:T(8,128)(2,1)}, u32[]{:S(2)}, u32[]{:S(2)}) %all-to-all-start.1) | async-done | bytes 4980768 | tf_op jit(solution)/shard_map/all_to_all | solution.py:217
  865.6 7.5 reshape.449
  873.1 12.0 gather_fusion
  885.0 4.9 fusion.74
  890.0 90.9 %all-to-all-done.3 = bf16[32,38,2048]{2,1,0:T(8,128)(2,1)} async-done(((bf16[32,38,2048]{2,1,0:T(8,128)(2,1)}), bf16[32,38,2048]{2,1,0:T(8,128)(2,1)}, u32[]{:S(2)}, u32[]{:S(2)}) %all-to-all-start.3) | async-done | bytes 4980768 | tf_op jit(solution)/shard_map/all_to_all | solution.py:274
  980.9 7.5 reshape.453
  988.4 12.2 gather_fusion.1
  1000.6 5.1 convert_reduce_fusion
  1009.1 11.4 fusion.121
  1021.8 26.5 %while.52 = (s32[]{:T(128)}, f32[4,8,128]{2,1,0:T(8,128)S(1)}, s32[4]{0:T(128)S(1)}, s32[]{:T(128)}, bf16[4,256,4,128]{3,1,2,0:T(8,128)(2,1)}, /*index=5*/bf16[1...) while((s32[]{:T(128)}, f32[4,8,128]{2,1,0:T(8,128)S(1)}, ...), condition=%wide.region_26.27_spmd.clone, body=%wide.region_24.26_spmd.clone.sunk | while | flops 542184320 | bytes 11162267 | solution.py:305
  1048.2 70.1 %while.53 = (s32[]{:T(128)}, f32[128,4,8,128]{0,3,2,1:T(8,128)}, bf16[4,256,4,128]{3,1,0,2:T(8,128)(2,1)}, bf16[4,256,4,128]{3,1,0,2:T(8,128)(2,1)}, bf16[4,256,...) while((s32[]{:T(128)}, f32[128,4,8,128]{0,3,2,1:T(8,128)}, ...), condition=%wide.region_28.29_spmd.clone, body=%wide.region_27.28_spmd.clone.sunk | while | flops 1353909120 | bytes 79583064 | solution.py:333
  1121.0 32.7 %reduce-scatter.14.cloned.1.call-done = bf16[128,4,128]{2,0,1:T(8,128)(2,1)} async-done(((bf16[1024,4,128]{2,0,1:T(8,128)(2,1)}), bf16[128,4,128]{2,0,1:T(8,128)(2,1)}) %reduce-scatter.14.cloned.1.call-update) | async-done | bytes 131088 | tf_op jit(solution)/shard_map/reduce_scatter | solution.py:339
  1173.1 19.5 %reduce-scatter.16.cloned.1.call-done = bf16[128,4,128]{2,0,1:T(8,128)(2,1)} async-done(((bf16[1024,4,128]{2,0,1:T(8,128)(2,1)}), bf16[128,4,128]{2,0,1:T(8,128)(2,1)}) %reduce-scatter.16.cloned.1.call-update) | async-done | bytes 131088 | tf_op jit(solution)/shard_map/reduce_scatter | solution.py:345
  1195.9 4.9 fusion.153
  1208.2 4.3 multiply_reduce_fusion
  1219.8 5.0 fusion.106
  1224.8 9.4 convolution_convert_fusion.1
  1235.8 8.2 convolution_convert_fusion
  1251.7 41.8 %reduce-scatter.22.cloned.1.call-done = bf16[2048,64]{0,1:T(8,128)(2,1)} async-done(((bf16[2048,512]{0,1:T(8,128)(2,1)}), bf16[2048,64]{0,1:T(8,128)(2,1)}) %reduce-scatter.22.cloned.1.call-update) | async-done | bytes 262160 | tf_op jit(solution)/shard_map/reduce_scatter | solution.py:398
  1293.5 44.4 %reduce-scatter.26.cloned.1.call-done = bf16[2048,64]{0,1:T(8,128)(2,1)} async-done(((bf16[2048,512]{0,1:T(8,128)(2,1)}), bf16[2048,64]{0,1:T(8,128)(2,1)}) %reduce-scatter.26.cloned.1.call-update) | async-done | bytes 262160 | tf_op jit(solution)/shard_map/reduce_scatter | solution.py:401
  1338.0 119.4 %reduce-scatter.18.cloned.1.call-done = bf16[2048,512]{1,0:T(8,128)(2,1)} async-done(((bf16[2048,4096]{1,0:T(8,128)(2,1)}), bf16[2048,512]{1,0:T(8,128)(2,1)}) %reduce-scatter.18.cloned.1.call-update) | async-done | bytes 2097168 | tf_op jit(solution)/shard_map/reduce_scatter | solution.py:395
  1457.4 9.2 convolution_bitcast_fusion.1
  1466.6 9.3 convolution_bitcast_fusion.2
  1475.9 100.9 %reduce-scatter.30.cloned.1.call-done = bf16[4096,256]{1,0:T(8,128)(2,1)} async-done(((bf16[4096,2048]{1,0:T(8,128)(2,1)}), bf16[4096,256]{1,0:T(8,128)(2,1)}) %reduce-scatter.30.cloned.1.call-update) | async-done | bytes 2097168 | tf_op jit(solution)/shard_map/reduce_scatter | solution.py:404
  1576.8 8.6 convolution_bitcast_fusion.3
  1585.5 12.5 fusion.156
  1607.5 39.2 %all-reduce.1 = (f32[2048]{0:T(1024)}, f32[2048]{0:T(1024)}, f32[128]{0:T(128)}, f32[128]{0:T(128)}) all-reduce(f32[2048]{0:T(1024)S(1)} %get-tuple-element.702, f32[2048]{0:T(1024)S(1)} %copy-done.44, f32[128]{0:T(128)S(1)} %copy-done.50, f32[128]{0:T(128)S(1)} %copy-done.49), channel_id=1, replica_groups=mesh['dp'=4,'expert'=8] {'dp','expert'}, use_global_device_ids=true, to_apply=%region_45.46 | all-reduce | flops 4352 | bytes 34816 | tf_op jit(solution)/shard_map/psum | solution.py:378
  1652.8 33.5 %reduce-scatter.20.cloned.1.call-done = bf16[512,512]{1,0:T(8,128)(2,1)} async-done(((bf16[2048,512]{1,0:T(8,128)(2,1)}), bf16[512,512]{1,0:T(8,128)(2,1)}) %reduce-scatter.20.cloned.1.call-update) | async-done | bytes 524304 | tf_op jit(solution)/shard_map/reduce_scatter | solution.py:412
  1688.5 42.9 %reduce-scatter.32.cloned.1.call-done = bf16[1024,256]{1,0:T(8,128)(2,1)} async-done(((bf16[4096,256]{1,0:T(8,128)(2,1)}), bf16[1024,256]{1,0:T(8,128)(2,1)}) %reduce-scatter.32.cloned.1.call-update) | async-done | bytes 524304 | tf_op jit(solution)/shard_map/reduce_scatter | solution.py:421
  (447 shorter events, 261.0 us)
Async XLA Ops:
  7.2 714.9 %copy-start = (bf16[1,768,2048]{2,1,0:T(8,128)(2,1)S(1)}, bf16[1,768,2048]{2,1,0:T(8,128)(2,1)}, u32[]{:S(2)}) copy-start(bf16[1,768,2048]{2,1,0:T(8,128)(2,1)} %param.38) | copy-start | bytes 9437188
  7.2 45.7 %all-gather.14.cloned.1.call-start = ((), (), s32[]{:S(2)}) async-start(), calls=%async_computation.17 | async-start | bytes 2359296 | tf_op jit(solution)/shard_map/all_gather | solution.py:88
  25.0 75.1 %all-gather.18.cloned.1.call-start = ((), (), s32[]{:S(2)}) async-start(), calls=%async_computation.19 | async-start | bytes 2621440 | tf_op jit(solution)/shard_map/all_gather | solution.py:80
  25.8 102.9 %all-gather.10.cloned.1.call-start = ((), (), s32[]{:S(2)}) async-start(), calls=%async_computation.15 | async-start | bytes 2359296 | tf_op jit(solution)/shard_map/all_gather | solution.py:89
  40.8 135.0 %all-gather.22.cloned.1.call-start = ((), (), s32[]{:S(2)}) async-start(), calls=%async_computation.21 | async-start | bytes 2621440 | tf_op jit(solution)/shard_map/all_gather | solution.py:83
  41.4 158.9 %all-gather.16.cloned.1.call-start = ((), (), s32[]{:S(2)}) async-start(), calls=%async_computation.18 | async-start | bytes 1179648 | tf_op jit(solution)/shard_map/all_gather | solution.py:122
  41.8 134.7 %copy-start.23 = (f32[128,128]{1,0:T(8,128)}, f32[128,128]{1,0:T(8,128)S(1)}, u32[]{:S(2)}) copy-start(f32[128,128]{1,0:T(8,128)S(1)} %pad_maximum_fusion.2) | copy-start | bytes 196612
  42.6 133.2 %copy-start.25 = (f32[128,128]{1,0:T(8,128)}, f32[128,128]{1,0:T(8,128)S(1)}, u32[]{:S(2)}) copy-start(f32[128,128]{1,0:T(8,128)S(1)} %get-tuple-element.807) | copy-start | bytes 196612
  43.8 251.3 %copy-start.42 = (f32[128]{0:T(128)}, f32[128]{0:T(128)S(1)}, u32[]{:S(2)}) copy-start(f32[128]{0:T(128)S(1)} %add_rsqrt_fusion.3) | copy-start | bytes 1540
  43.8 84.8 %copy-start.32 = (f32[2048]{0:T(1024)S(1)}, f32[2048]{0:T(1024)}, u32[]{:S(2)}) copy-start(f32[2048]{0:T(1024)} %param.32) | copy-start | bytes 24580
  55.5 75.8 %copy-start.15 = (f32[128,512]{1,0:T(8,128)}, f32[128,512]{1,0:T(8,128)S(1)}, u32[]{:S(2)}) copy-start(f32[128,512]{1,0:T(8,128)S(1)} %fusion.149) | copy-start | bytes 786436
  61.5 115.2 %copy-start.39 = (s32[128,8]{0,1:T(8,128)S(1)}, s32[128,8]{0,1:T(8,128)}, u32[]{:S(2)}) copy-start(s32[128,8]{0,1:T(8,128)} %param.25) | copy-start | bytes 12292
  61.5 233.6 %all-gather.20.cloned.1.call-start = ((), (), s32[]{:S(2)}) async-start(), calls=%async_computation.20 | async-start | bytes 18874368 | tf_op jit(solution)/shard_map/all_gather | solution.py:87
  100.2 255.6 %all-gather.12.cloned.1.call-start = ((), (), s32[]{:S(2)}) async-start(), calls=%async_computation.16 | async-start | bytes 1179648 | tf_op jit(solution)/shard_map/all_gather | solution.py:123
  132.0 283.9 %all-gather.24.cloned.1.call-start = ((), (), s32[]{:S(2)}) async-start(), calls=%async_computation.22 | async-start | bytes 18874368 | tf_op jit(solution)/shard_map/all_gather | solution.py:90
  304.8 4.8 copy-start.45
  415.9 9.5 copy-start.38
  444.2 4.7 copy-start.48
  444.2 157.2 %all-to-all-start = ((bf16[32,38,2048]{2,1,0:T(8,128)(2,1)}), bf16[32,38,2048]{2,1,0:T(8,128)(2,1)}, u32[]{:S(2)}, u32[]{:S(2)}) async-start(bf16[32,38,2048]{2,1,0:T(8,128)(2,1)} %reshape.444), calls=%async_computation | async-start | bytes 10485760 | tf_op jit(solution)/shard_map/all_to_all | solution.py:200
  601.4 120.7 %all-to-all-start.2 = ((bf16[32,38,2048]{2,1,0:T(8,128)(2,1)}), bf16[32,38,2048]{2,1,0:T(8,128)(2,1)}, u32[]{:S(2)}, u32[]{:S(2)}) async-start(bf16[32,38,2048]{2,1,0:T(8,128)(2,1)} %reshape.450), calls=%async_computation.2 | async-start | bytes 10485760 | tf_op jit(solution)/shard_map/all_to_all | solution.py:248
  605.5 9.8 copy-start.52
  740.1 120.4 %all-to-all-start.1 = ((bf16[32,38,2048]{2,1,0:T(8,128)(2,1)}), bf16[32,38,2048]{2,1,0:T(8,128)(2,1)}, u32[]{:S(2)}, u32[]{:S(2)}) async-start(bf16[32,38,2048]{2,1,0:T(8,128)(2,1)} %convolution_convert_fusion.3), calls=%async_computation.1 | async-start | bytes 10485760 | tf_op jit(solution)/shard_map/all_to_all | solution.py:217
  744.1 6.1 copy-start.53
  758.0 106.5 %copy-start.27 = (bf16[4,256,4,128]{3,1,0,2:T(8,128)(2,1)S(1)}, bf16[4,256,4,128]{3,1,0,2:T(8,128)(2,1)}, u32[]{:S(2)}) copy-start(bf16[4,256,4,128]{3,1,0,2:T(8,128)(2,1)} %get-tuple-element.1273) | copy-start | bytes 3145732
  860.5 120.4 %all-to-all-start.3 = ((bf16[32,38,2048]{2,1,0:T(8,128)(2,1)}), bf16[32,38,2048]{2,1,0:T(8,128)(2,1)}, u32[]{:S(2)}, u32[]{:S(2)}) async-start(bf16[32,38,2048]{2,1,0:T(8,128)(2,1)} %add_convert_fusion), calls=%async_computation.3 | async-start | bytes 10485760 | tf_op jit(solution)/shard_map/all_to_all | solution.py:274
  864.4 289.2 %reduce-scatter.14.cloned.1.call-start = ((), (), s32[]{:S(2)}) async-start(), calls=%async_computation.23 | async-start | bytes 1179648 | tf_op jit(solution)/shard_map/reduce_scatter | solution.py:339
  873.1 12.0 copy-start.14
  1000.6 5.2 copy-start.12
  1000.6 6.2 copy-start.21
  1048.2 105.4 %copy-start.24 = (f32[128,128]{1,0:T(8,128)S(1)}, f32[128,128]{1,0:T(8,128)}, u32[]{:S(2)}) copy-start(f32[128,128]{1,0:T(8,128)} %copy-done.23) | copy-start | bytes 196612
  1057.6 4.8 copy-start.4
  1074.5 5.5 copy-start.4
  1092.1 5.5 copy-start.4
  1109.8 5.5 copy-start.4
  1118.3 36.4 %copy-start.16 = (f32[128,512]{1,0:T(8,128)S(1)}, f32[128,512]{1,0:T(8,128)}, u32[]{:S(2)}) copy-start(f32[128,512]{1,0:T(8,128)} %copy-done.15) | copy-start | bytes 786436
  1118.3 36.5 %copy-start.26 = (f32[128,128]{1,0:T(8,128)S(1)}, f32[128,128]{1,0:T(8,128)}, u32[]{:S(2)}) copy-start(f32[128,128]{1,0:T(8,128)} %copy-done.25) | copy-start | bytes 196612
  1118.3 36.5 %copy-start.41 = (f32[128,4]{0,1:T(4,128)S(1)}, f32[128,4]{0,1:T(4,128)}, u32[]{:S(2)}) copy-start(f32[128,4]{0,1:T(4,128)} %copy-done.40) | copy-start | bytes 6148
  1118.3 36.5 %copy-start.47 = (f32[128]{0:T(128)S(1)}, f32[128]{0:T(128)}, u32[]{:S(2)}) copy-start(f32[128]{0:T(128)} %param.35) | copy-start | bytes 1540
  1118.3 38.5 %copy-start.7 = (bf16[128,2048]{1,0:T(8,128)(2,1)S(1)}, bf16[128,2048]{1,0:T(8,128)(2,1)}, u32[]{:S(2)}) copy-start(bf16[128,2048]{1,0:T(8,128)(2,1)} %param.24) | copy-start | bytes 1572868
  1118.3 38.5 %copy-start.33 = (f32[2048]{0:T(1024)S(1)}, f32[2048]{0:T(1024)}, u32[]{:S(2)}) copy-start(f32[2048]{0:T(1024)} %param.32) | copy-start | bytes 24580
  1118.3 38.5 %copy-start.43 = (f32[128]{0:T(128)S(1)}, f32[128]{0:T(128)}, u32[]{:S(2)}) copy-start(f32[128]{0:T(128)} %copy-done.42) | copy-start | bytes 1540
  1118.4 74.3 %reduce-scatter.16.cloned.1.call-start = ((), (), s32[]{:S(2)}) async-start(), calls=%async_computation.24 | async-start | bytes 1179648 | tf_op jit(solution)/shard_map/reduce_scatter | solution.py:345
  1119.0 130.8 %all-reduce.4.cloned.1.call-start = ((), (), s32[]{:S(2)}) async-start(), calls=%async_computation.34 | async-start | bytes 262144
  1120.9 172.5 %reduce-scatter.22.cloned.1.call-start = ((), (), s32[]{:S(2)}) async-start(), calls=%async_computation.27 | async-start | bytes 2359296 | tf_op jit(solution)/shard_map/reduce_scatter | solution.py:398
  1154.6 5.5 copy-start.46
  1159.0 6.2 copy-start.5
  1159.0 178.9 %reduce-scatter.26.cloned.1.call-start = ((), (), s32[]{:S(2)}) async-start(), calls=%async_computation.29 | async-start | bytes 2359296 | tf_op jit(solution)/shard_map/reduce_scatter | solution.py:401
  1195.9 261.5 %reduce-scatter.18.cloned.1.call-start = ((), (), s32[]{:S(2)}) async-start(), calls=%async_computation.25 | async-start | bytes 18874368 | tf_op jit(solution)/shard_map/reduce_scatter | solution.py:395
  1200.9 7.3 copy-start.36
  1234.2 342.5 %reduce-scatter.30.cloned.1.call-start = ((), (), s32[]{:S(2)}) async-start(), calls=%async_computation.31 | async-start | bytes 18874368 | tf_op jit(solution)/shard_map/reduce_scatter | solution.py:404
  1243.9 213.5 %copy-start.57 = (bf16[32,1,38,768]{3,2,0,1:T(8,128)(2,1)S(1)}, bf16[32,1,38,768]{3,2,0,1:T(8,128)(2,1)}, u32[]{:S(2)}) copy-start(bf16[32,1,38,768]{3,2,0,1:T(8,128)(2,1)} %copy-done.56) | copy-start | bytes 5603332
  1243.9 357.4 %reduce-scatter.34.cloned.1.call-start = ((), (), s32[]{:S(2)}) async-start(), calls=%async_computation.33 | async-start | bytes 655360
  1251.6 398.1 %reduce-scatter.24.cloned.1.call-start = ((), (), s32[]{:S(2)}) async-start(), calls=%async_computation.28 | async-start | bytes 327680 | tf_op jit(solution)/shard_map/reduce_scatter | solution.py:415
  1293.5 357.8 %reduce-scatter.28.cloned.1.call-start = ((), (), s32[]{:S(2)}) async-start(), calls=%async_computation.30 | async-start | bytes 327680 | tf_op jit(solution)/shard_map/reduce_scatter | solution.py:418
  1337.9 348.4 %reduce-scatter.20.cloned.1.call-start = ((), (), s32[]{:S(2)}) async-start(), calls=%async_computation.26 | async-start | bytes 2621440 | tf_op jit(solution)/shard_map/reduce_scatter | solution.py:412
  1457.4 274.0 %reduce-scatter.32.cloned.1.call-start = ((), (), s32[]{:S(2)}) async-start(), calls=%async_computation.32 | async-start | bytes 2621440 | tf_op jit(solution)/shard_map/reduce_scatter | solution.py:421
  1457.4 9.2 copy-start.58
  1466.6 110.2 %copy-start.59 = (bf16[32,1,38,768]{3,2,0,1:T(8,128)(2,1)S(1)}, bf16[32,1,38,768]{3,2,0,1:T(8,128)(2,1)}, u32[]{:S(2)}) copy-start(bf16[32,1,38,768]{3,2,0,1:T(8,128)(2,1)} %get-tuple-element.794) | copy-start | bytes 5603332
  1576.8 8.7 copy-start.17
  1585.5 17.5 %copy-start.18 = (bf16[2048,512]{0,1:T(8,128)(2,1)S(1)}, bf16[2048,512]{0,1:T(8,128)(2,1)}, u32[]{:S(2)}) copy-start(bf16[2048,512]{0,1:T(8,128)(2,1)} %all-gather.14.cloned.1.call-done) | copy-start | bytes 6291460
  1603.0 4.6 copy-start.44
  1603.0 4.6 copy-start.49
  1603.0 4.6 copy-start.50
  1604.8 128.7 %copy-start.1 = (bf16[1,768,2048]{2,1,0:T(8,128)(2,1)S(1)}, bf16[1,768,2048]{2,1,0:T(8,128)(2,1)}, u32[]{:S(2)}) copy-start(bf16[1,768,2048]{2,1,0:T(8,128)(2,1)} %param.38) | copy-start | bytes 9437188
  (38 other events, 96.2 us)
Sparse Core Ops, SparseCore 0:
  25.1 27.7 all-gather.13
  54.4 45.6 all-gather.17
  102.0 26.5 all-gather.9
  130.1 45.6 all-gather.21
  178.1 22.1 all-gather.15
  202.0 93.0 all-gather.19
  297.6 23.3 all-gather.11
  322.8 93.0 all-gather.23
  1118.5 35.1 reduce-scatter.13
  1156.7 35.9 reduce-scatter.15
  1196.3 53.4 all-reduce.3
  1252.9 40.4 reduce-scatter.21
  1296.7 41.1 reduce-scatter.25
  1341.3 115.9 reduce-scatter.17
  1460.8 115.9 reduce-scatter.29
  1579.5 21.8 reduce-scatter.33
  1603.5 18.2 reduce-scatter.23
  1623.9 18.1 reduce-scatter.27
  1644.3 41.9 reduce-scatter.19
  1688.4 42.8 reduce-scatter.31
where the time goes:
time: 1750 us; the launch traced here: 1740 us
  waiting for transfers between devices  989 us (57%)
  matrix products  251 us (14%)
  blocking collectives  203 us (12%)
  other arithmetic  132 us (8%)
  local copies, waits for them, and re-layouts  131 us (7%)
  starting transfers between devices  17.7 us (1%)
    all_gather x1, blocking collectives, shards(): lax.all_gather(router_weight, 'dp', axis=0, tiled=True)  122 us
    reduce_scatter x1, waiting for transfers between devices, shards(): lax.psum_scatter(query_gradient.astype(jnp.bfloat16), 'expert', scatter_d...  119 us
    all_to_all x1, waiting for transfers between devices, shards(): lax.all_to_all(produced.reshape(devices, EXP_DEV * capacity, MODEL_WIDTH)...  102 us
    reduce_scatter x1, waiting for transfers between devices, shards(): lax.psum_scatter(out_gradient.astype(jnp.bfloat16), 'expert', scatter_dim...  101 us
    all_to_all x1, waiting for transfers between devices, shards(): lax.all_to_all(outgoing_grad.reshape(devices, EXP_DEV * capacity, MODEL_W...  97.9 us
    all_gather x1, waiting for transfers between devices, shards(): lax.all_gather(query_rows, 'expert', axis=1, tiled=True)  92.5 us
    all_to_all x1, waiting for transfers between devices, shards(): lax.all_to_all(row_grad.reshape(devices, EXP_DEV * capacity, MODEL_WIDTH)...  90.9 us
    reduce_scatter x1, waiting for transfers between devices, shards(): lax.psum_scatter(value_gradient.astype(jnp.bfloat16), 'expert', scatter_d...  44.4 us
  transfers between devices with their start and end apart: 24, of which 20 were waited for; matrix products, arithmetic and copies ran while one was open for 19% of the time, Pallas kernels for 0%

commit v1 on v0

v1 whole, which is shorter than its diff:
```python
import jax
import jax.numpy as jnp
from jax import lax
from jax.experimental import pallas as pl
from jax.experimental.pallas import tpu as pltpu
from jax.sharding import PartitionSpec as P

QUERY_HEADS = 32
KEY_VALUE_HEADS = 4
HEAD_SIZE = 128
TOP = 8
EPS = 1e-06
ROTARY_BASE = 1000000.0
VERY_NEGATIVE = -1e30
SCALE = HEAD_SIZE ** (-0.5)
F32 = jnp.float32
BF16 = jnp.bfloat16
BOTH = ("dp", "expert")


def dot(a, b, dims=((1,), (0,))):
    return lax.dot_general(a, b, (dims, ((), ())), preferred_element_type=F32)


def scale_of(u):
    return lax.rsqrt(jnp.mean(u * u, axis=-1, keepdims=True) + EPS)


def norm_back(upstream, unit, scaling, gain):
    weighted = upstream * gain
    return scaling * (weighted - unit * jnp.mean(weighted * unit, axis=-1, keepdims=True))


def rotary_tables(span):
    half = HEAD_SIZE // 2
    frequency = jnp.power(ROTARY_BASE, -jnp.arange(half, dtype=F32) * 2.0 / HEAD_SIZE)
    angles = jnp.arange(span, dtype=jnp.int32).astype(F32)[:, None] * frequency[None, :]
    cosine, sine = jnp.cos(angles), jnp.sin(angles)
    return jnp.concatenate([cosine, cosine], axis=-1), jnp.concatenate([-sine, sine], axis=-1)


def rope(u, cosine, sine):
    return u * cosine + pltpu.roll(u, HEAD_SIZE // 2, 1) * sine


def rope_back(g, cosine, sine):
    return g * cosine - pltpu.roll(g, HEAD_SIZE // 2, 1) * sine


def block_spans(span):
    rows = min(256, span)
    return [(at, rows, max(at + rows, span // 2)) for at in range(0, span, rows)]


def allowed_of(at, rows, keys, prefix):
    key_place = lax.broadcasted_iota(jnp.int32, (keys, rows), 0)
    query_place = at + lax.broadcasted_iota(jnp.int32, (keys, rows), 1)
    return (key_place <= query_place) | (key_place < prefix)


def attend_kernel(
    prefix_ref, q_ref, k_ref, v_ref, qgain_ref, kgain_ref, cos_ref, sin_ref,
    out_ref, lse_ref, qlow_ref, klow, vturned,
):
    span = q_ref.shape[0]
    prefix = prefix_ref[0]

    @pl.when(pl.program_id(0) == 0)
    def _():
        k = k_ref[...]
        klow[...] = rope(k * scale_of(k) * kgain_ref[...], cos_ref[...], sin_ref[...]).astype(BF16)
        vturned[...] = v_ref[...].T.astype(BF16)

    q = q_ref[...]
    qlow_ref[...] = rope(q * scale_of(q) * qgain_ref[...], cos_ref[...], sin_ref[...]).astype(BF16)
    for at, rows, keys in block_spans(span):
        qlow = qlow_ref[at : at + rows, :]
        scores = dot(klow[:keys, :], qlow, ((1,), (1,))) * SCALE
        scores = jnp.where(allowed_of(at, rows, keys, prefix), scores, VERY_NEGATIVE)
        high = jnp.max(scores, axis=0, keepdims=True)
        weights = jnp.exp(scores - high)
        total = jnp.sum(weights, axis=0, keepdims=True)
        weights_low = (weights * (1.0 / total)).astype(BF16)
        out = dot(vturned[:, :keys], weights_low)
        out_ref[at : at + rows, :] = out.T.astype(BF16)
        lse_ref[0, :, at : at + rows] = high + jnp.log(total)


def attend(prefix, qkv, heads, qgain, kgain, cosine, sine):
    span = qkv.shape[0]
    whole = lambda h: (0, 0)
    column = lambda index: pl.BlockSpec((span, HEAD_SIZE), index)
    keys = sum(rows * keys for _, rows, keys in block_spans(span))
    return pl.pallas_call(
        attend_kernel,
        grid=(heads,),
        in_specs=[
            pl.BlockSpec(memory_space=pltpu.SMEM),
            column(lambda h: (0, h)),
            column(lambda h: (0, heads)),
            column(lambda h: (0, heads + 1)),
            pl.BlockSpec((1, HEAD_SIZE), whole),
            pl.BlockSpec((1, HEAD_SIZE), whole),
            column(whole),
            column(whole),
        ],
        out_specs=[
            column(lambda h: (0, h)),
            pl.BlockSpec((1, 1, span), lambda h: (h, 0, 0)),
            column(lambda h: (0, h)),
        ],
        out_shape=[
            jax.ShapeDtypeStruct((span, heads * HEAD_SIZE), BF16),
            jax.ShapeDtypeStruct((heads, 1, span), F32),
            jax.ShapeDtypeStruct((span, heads * HEAD_SIZE), BF16),
        ],
        scratch_shapes=[
            pltpu.VMEM((span, HEAD_SIZE), BF16),
            pltpu.VMEM((HEAD_SIZE, span), BF16),
        ],
        cost_estimate=pl.CostEstimate(
            flops=4 * heads * keys * HEAD_SIZE,
            bytes_accessed=span * HEAD_SIZE * (8 * heads + 16),
            transcendentals=heads * keys,
        ),
        compiler_params=pltpu.CompilerParams(vmem_limit_bytes=40 * 1024 * 1024),
        name="attend",
    )(prefix, qkv, qkv, qkv, qgain, kgain, cosine, sine)


def attend_back_kernel(
    prefix_ref, q_ref, k_ref, v_ref, qlow_ref, lse_ref, up_ref,
    qgain_ref, kgain_ref, cos_ref, sin_ref,
    dq_ref, dkv_ref, qterm_ref, kterm_ref,
    klow, kturned, vlow, dk, dv, dq,
):
    span = q_ref.shape[0]
    prefix = prefix_ref[0]
    head = pl.program_id(0)

    @pl.when(head == 0)
    def _():
        k = k_ref[...]
        low = rope(k * scale_of(k) * kgain_ref[...], cos_ref[...], sin_ref[...])
        klow[...] = low.astype(BF16)
        kturned[...] = low.T.astype(BF16)
        vlow[...] = v_ref[...].astype(BF16)
        dk[...] = jnp.zeros_like(dk)
        dv[...] = jnp.zeros_like(dv)
        qterm_ref[...] = jnp.zeros_like(qterm_ref)

    for at, rows, keys in block_spans(span):
        qlow = qlow_ref[at : at + rows, :]
        up = up_ref[at : at + rows, :]
        scores = dot(klow[:keys, :], qlow, ((1,), (1,))) * SCALE
        allowed = allowed_of(at, rows, keys, prefix)
        weights = jnp.where(allowed, jnp.exp(scores - lse_ref[0, :, at : at + rows]), 0.0)
        weight_grad = dot(vlow[:keys, :], up, ((1,), (1,)))
        delta = jnp.sum(weights * weight_grad, axis=0, keepdims=True)
        score_grad = (weights * (weight_grad - delta)).astype(BF16)
        dv[:keys, :] += dot(weights.astype(BF16), up)
        dk[:keys, :] += dot(score_grad, qlow)
        dq[at : at + rows, :] = dot(kturned[:, :keys], score_grad).T

    q = q_ref[...]
    scaling = scale_of(q)
    unit = q * scaling
    turned = rope_back(dq[...] * SCALE, cos_ref[...], sin_ref[...])
    qterm_ref[...] += jnp.sum(turned * unit, axis=0, keepdims=True)
    dq_ref[...] = norm_back(turned, unit, scaling, qgain_ref[...]).astype(BF16)

    @pl.when(head == pl.num_programs(0) - 1)
    def _():
        k = k_ref[...]
        unit = k * scale_of(k)
        turned = rope_back(dk[...] * SCALE, cos_ref[...], sin_ref[...])
        kterm_ref[...] = jnp.sum(turned * unit, axis=0, keepdims=True)
        dkv_ref[:, :HEAD_SIZE] = turned.astype(BF16)
        dkv_ref[:, HEAD_SIZE:] = dv[...].astype(BF16)


def attend_back(prefix, qkv, heads, qlow, lse, upstream, qgain, kgain, cosine, sine):
    span = qkv.shape[0]
    whole = lambda h: (0, 0)
    column = lambda index: pl.BlockSpec((span, HEAD_SIZE), index)
    row = pl.BlockSpec((1, HEAD_SIZE), whole)
    keys = sum(rows * keys for _, rows, keys in block_spans(span))
    return pl.pallas_call(
        attend_back_kernel,
        grid=(heads,),
        in_specs=[
            pl.BlockSpec(memory_space=pltpu.SMEM),
            column(lambda h: (0, h)),
            column(lambda h: (0, heads)),
            column(lambda h: (0, heads + 1)),
            column(lambda h: (0, h)),
            pl.BlockSpec((1, 1, span), lambda h: (h, 0, 0)),
            column(lambda h: (0, h)),
            row,
            row,
            column(whole),
            column(whole),
        ],
        out_specs=[
            column(lambda h: (0, h)),
            pl.BlockSpec((span, 2 * HEAD_SIZE), whole),
            row,
            row,
        ],
        out_shape=[
            jax.ShapeDtypeStruct((span, heads * HEAD_SIZE), BF16),
            jax.ShapeDtypeStruct((span, 2 * HEAD_SIZE), BF16),
            jax.ShapeDtypeStruct((1, HEAD_SIZE), F32),
            jax.ShapeDtypeStruct((1, HEAD_SIZE), F32),
        ],
        scratch_shapes=[
            pltpu.VMEM((span, HEAD_SIZE), BF16),
            pltpu.VMEM((HEAD_SIZE, span), BF16),
            pltpu.VMEM((span, HEAD_SIZE), BF16),
            pltpu.VMEM((span, HEAD_SIZE), F32),
            pltpu.VMEM((span, HEAD_SIZE), F32),
            pltpu.VMEM((span, HEAD_SIZE), F32),
        ],
        cost_estimate=pl.CostEstimate(
            flops=10 * heads * keys * HEAD_SIZE,
            bytes_accessed=span * HEAD_SIZE * (10 * heads + 16),
            transcendentals=heads * keys,
        ),
        compiler_params=pltpu.CompilerParams(vmem_limit_bytes=48 * 1024 * 1024),
        name="attend_back",
    )(prefix, qkv, qkv, qkv, qlow, lse, upstream, qgain, kgain, cosine, sine)


def exchange(x, axes):
    return lax.all_to_all(x, axes, split_axis=0, concat_axis=0, tiled=True)


def shards(
    tokens,
    routes,
    prefix_len,
    query_weight,
    key_matrix,
    value_matrix,
    out_weight,
    router_weight,
    attention_gain,
    mixture_gain,
    query_gain,
    key_norm_gain,
    expert_gate,
    expert_up,
    expert_down,
    cotangent,
):
    planes = lax.axis_size("dp")
    lanes = lax.axis_size("expert")
    plane = lax.axis_index("dp")
    lane = lax.axis_index("expert")
    devices = planes * lanes
    resident, width = tokens.shape
    span = lanes * resident
    group = planes * resident
    columns = query_weight.shape[1]
    heads = columns // HEAD_SIZE
    narrow = key_matrix.shape[1]
    sharers = lanes // KEY_VALUE_HEADS
    member = lane % sharers
    experts = router_weight.shape[1] * lanes
    own_expert = plane * lanes + lane
    slots = planes * max(2, 6 * resident * TOP // (5 * experts))

    def to_all(x):
        return exchange(jnp.broadcast_to(x[None], (devices,) + x.shape), BOTH)

    def from_member(x, step):
        pairs = [(i, i - i % sharers + (i + step) % sharers) for i in range(lanes)]
        return lax.ppermute(x, "expert", pairs)

    residual = tokens.astype(F32)
    scaling_in = scale_of(residual)
    unit_in = residual * scaling_in
    normed = lax.all_gather(
        (unit_in * attention_gain).astype(BF16), "expert", axis=0, tiled=True
    )

    projection = lax.all_gather(
        jnp.concatenate([query_weight, key_matrix, value_matrix], axis=1), "dp", axis=0, tiled=True
    )
    turns = [projection[:, columns:]]
    turns += [from_member(turns[0], step) for step in range(1, sharers)]
    ordered = []
    for place in range(sharers):
        step_of = (member - place) % sharers
        piece = turns[0]
        for step in range(1, sharers):
            piece = jnp.where(step_of == step, turns[step], piece)
        ordered.append(piece)
    wide = jnp.concatenate(
        [projection[:, :columns]]
        + [piece[:, :narrow] for piece in ordered]
        + [piece[:, narrow:] for piece in ordered],
        axis=1,
    )
    out_rows = lax.all_gather(out_weight, "dp", axis=0, tiled=True)
    out_rows = lax.all_to_all(
        out_rows.reshape(lanes, columns, out_weight.shape[1]),
        "expert", split_axis=0, concat_axis=2, tiled=True,
    ).reshape(columns, width)

    expert_ids = jnp.arange(experts, dtype=jnp.int32)
    mask_turned = jnp.sum(
        (routes.T[:, None, :] == expert_ids[None, :, None]).astype(F32), axis=0
    )
    mask = mask_turned.T
    masks = to_all(mask_turned.astype(BF16)).reshape(planes, lanes, experts, resident)
    earlier = (
        lax.broadcasted_iota(jnp.int32, (group, group), 0)
        < lax.broadcasted_iota(jnp.int32, (group, group), 1)
    ).astype(BF16)
    slot_ids = lax.broadcasted_iota(jnp.int32, (1, slots, 1), 1)

    def slot_table(chosen):
        rank = dot(chosen, earlier).astype(jnp.int32)
        rank = jnp.where(chosen > 0, rank, -1)
        return (rank[:, None, :] == slot_ids).astype(BF16)

    send_mask = lax.dynamic_slice_in_dim(
        lax.dynamic_index_in_dim(masks, lane, 1, keepdims=False), plane * lanes, lanes, 1
    )
    send_table = slot_table(send_mask.transpose(1, 0, 2).reshape(lanes, group))
    send_rows = send_table.reshape(lanes * slots, group)
    here_mask = lax.dynamic_index_in_dim(masks, own_expert, 2, keepdims=False)
    here_table = slot_table(here_mask.transpose(1, 0, 2).reshape(lanes, group))
    row_mask = jnp.einsum(
        "lspr,plxr->lsx",
        here_table.reshape(lanes, slots, planes, resident),
        masks,
        preferred_element_type=F32,
    ).reshape(lanes * slots, experts)
    router_turned = (
        to_all(router_weight.T)
        .reshape(planes, lanes, experts // lanes, width // planes)
        .transpose(1, 2, 0, 3)
        .reshape(experts, width)
    )

    def dispatch(rows):
        gathered = lax.all_gather(rows, "dp", axis=0, tiled=True)
        placed = dot(send_rows, gathered).astype(BF16)
        return exchange(placed.reshape(lanes, slots, width), "expert").reshape(
            lanes * slots, width
        )

    def collect(rows):
        arrived = exchange(rows.reshape(lanes, slots, width), "expert")
        summed = dot(send_rows, arrived.reshape(lanes * slots, width), ((0,), (0,)))
        return lax.psum_scatter(
            summed.astype(BF16), "dp", scatter_dimension=0, tiled=True
        ).astype(F32)

    upstream_rows = dispatch(cotangent)

    prefix = prefix_len.astype(jnp.int32)
    cosine, sine = rotary_tables(span)
    qgain, kgain = query_gain[None, :], key_norm_gain[None, :]
    qkv = dot(normed, wide)
    attended, lse, qlow = attend(prefix, qkv, heads, qgain, kgain, cosine, sine)
    mixed_out = lax.psum_scatter(
        dot(attended, out_rows).astype(BF16), "expert", scatter_dimension=0, tiled=True
    )
    after_attn = residual + mixed_out.astype(F32)
    scaling_mix = scale_of(after_attn)
    unit_mix = after_attn * scaling_mix
    mixed_low = (unit_mix * mixture_gain).astype(BF16)

    rows = dispatch(mixed_low)

    def chosen_softmax(logits, chosen):
        logits = jnp.where(chosen > 0, logits, VERY_NEGATIVE)
        high = jnp.max(logits, axis=-1, keepdims=True)
        weights = jnp.where(chosen > 0, jnp.exp(logits - high), 0.0)
        return weights / jnp.maximum(jnp.sum(weights, axis=-1, keepdims=True), 1e-30)

    row_weights = chosen_softmax(dot(rows, router_turned, ((1,), (1,))), row_mask)
    row_weight = jnp.sum(
        jnp.where(expert_ids[None, :] == own_expert, row_weights, 0.0), axis=-1, keepdims=True
    )
    gate_matrix, up_matrix, down_matrix = expert_gate[0], expert_up[0], expert_down[0]
    gate_raw = dot(rows, gate_matrix)
    up_raw = dot(rows, up_matrix)
    gate_sig = jax.nn.sigmoid(gate_raw)
    activated = (gate_raw * gate_sig * up_raw).astype(BF16)
    produced_grad = (row_weight * upstream_rows.astype(F32)).astype(BF16)
    activated_grad = dot(produced_grad, down_matrix, ((1,), (1,)))
    gate_grad = (activated_grad * up_raw * gate_sig * (1.0 + gate_raw * (1.0 - gate_sig))).astype(
        BF16
    )
    up_grad = (activated_grad * gate_raw * gate_sig).astype(BF16)
    row_grad = (
        dot(gate_grad, gate_matrix, ((1,), (1,))) + dot(up_grad, up_matrix, ((1,), (1,)))
    ).astype(BF16)
    rows_back = collect(row_grad)

    produced = dot(activated, down_matrix).astype(BF16).astype(F32)
    route_rows = jnp.sum(produced * upstream_rows.astype(F32), axis=-1)
    route_dense = jnp.sum(
        here_table.astype(F32) * route_rows.reshape(lanes, slots)[:, :, None], axis=1
    )
    route_grad = exchange(
        route_dense.reshape(lanes, planes, resident).transpose(1, 0, 2).reshape(devices, resident),
        BOTH,
    ).T
    down_gradient = dot(activated, produced_grad, ((0,), (0,)))
    gate_gradient = dot(rows, gate_grad, ((0,), (0,)))
    up_gradient = dot(rows, up_grad, ((0,), (0,)))
    mixture = collect((row_weight * produced).astype(BF16))
    layer_out = (after_attn + mixture).astype(BF16)

    weight = chosen_softmax(dot(mixed_low, router_turned, ((1,), (1,))), mask)
    logit_grad = (
        weight * (route_grad - jnp.sum(weight * route_grad, axis=-1, keepdims=True))
    ).astype(BF16)
    upstream = cotangent.astype(F32)
    mixed_grad = dot(logit_grad, router_turned) + rows_back
    mixture_terms = jnp.sum(mixed_grad * unit_mix, axis=0)
    after_grad = upstream + norm_back(mixed_grad, unit_mix, scaling_mix, mixture_gain)
    after_low = lax.all_gather(after_grad.astype(BF16), "expert", axis=0, tiled=True)

    attended_grad = dot(after_low, out_rows, ((1,), (1,))).astype(BF16)
    dq, dkv, qterm, kterm = attend_back(
        prefix, qkv, heads, qlow, lse, attended_grad, qgain, kgain, cosine, sine
    )
    dkv_sum = dkv.astype(F32)
    for step in range(1, sharers):
        dkv_sum = dkv_sum + from_member(dkv, step).astype(F32)
    key_raw = qkv[:, columns : columns + HEAD_SIZE]
    scaling_key = scale_of(key_raw)
    key_back = norm_back(
        dkv_sum[:, :HEAD_SIZE], key_raw * scaling_key, scaling_key, kgain
    ).astype(BF16)
    value_back = dkv_sum[:, HEAD_SIZE:].astype(BF16)

    def own_columns(x):
        own = x[:, :narrow]
        for place in range(1, sharers):
            own = jnp.where(member == place, x[:, place * narrow : (place + 1) * narrow], own)
        return own

    back = jnp.concatenate([dq, own_columns(key_back), own_columns(value_back)], axis=1)
    normed_part = dot(back, projection, ((1,), (1,)))
    attention_terms = jnp.sum(normed_part * normed.astype(F32), axis=0) / attention_gain
    normed_grad = lax.psum_scatter(
        normed_part.astype(BF16), "expert", scatter_dimension=0, tiled=True
    ).astype(F32)
    input_grad = after_grad + norm_back(normed_grad, unit_in, scaling_in, attention_gain)

    projection_share = lax.psum_scatter(
        dot(normed, back, ((0,), (0,))).astype(BF16), "dp", scatter_dimension=0, tiled=True
    ).astype(F32)
    out_part = dot(attended, after_low, ((0,), (0,))).astype(BF16)
    out_part = lax.all_to_all(
        out_part.reshape(1, columns, width), "expert", split_axis=2, concat_axis=0, tiled=True
    ).reshape(lanes * columns, width // lanes)
    out_share = lax.psum_scatter(out_part, "dp", scatter_dimension=0, tiled=True).astype(F32)
    router_part = dot(logit_grad, mixed_low, ((0,), (0,))).astype(BF16)
    router_part = exchange(
        router_part.reshape(lanes, experts // lanes, planes, width // planes)
        .transpose(2, 0, 1, 3)
        .reshape(devices, experts // lanes, width // planes),
        BOTH,
    )
    router_share = jnp.sum(router_part.astype(F32), axis=0).T

    terms = jnp.concatenate([attention_terms, mixture_terms, qterm[0], kterm[0]]).reshape(
        -1, HEAD_SIZE
    )
    totals = jnp.sum(to_all(terms), axis=0).reshape(-1)
    return (
        layer_out,
        input_grad,
        projection_share[:, :columns],
        projection_share[:, columns : columns + narrow],
        projection_share[:, columns + narrow :],
        out_share,
        router_share,
        totals[:width],
        totals[width : 2 * width],
        totals[2 * width : 2 * width + HEAD_SIZE],
        totals[2 * width + HEAD_SIZE :],
        gate_gradient[None],
        up_gradient[None],
        down_gradient[None],
    )


def solution(mesh):
    rows = P(BOTH, None)
    block = P("dp", "expert")
    stack = P(BOTH, None, None)
    in_specs = (
        rows, rows, P("dp"), block, block, block, block, block,
        P(), P(), P(), P(), stack, stack, stack, rows,
    )
    out_specs = (
        rows, rows, block, block, block, block, block,
        P(), P(), P(), P(), stack, stack, stack,
    )
    return jax.shard_map(shards, mesh=mesh, in_specs=in_specs, out_specs=out_specs, check_vma=False)
```

time: 1750 us -> 867 us (0.50)
  waiting for transfers between devices: 989 us -> 373 us
  matrix products: 251 us -> 145 us
  other arithmetic: 132 us -> 45.7 us
  local copies, waits for them, and re-layouts: 131 us -> 58.6 us
  blocking collectives: 203 us -> 151 us
  Pallas kernels: 0 us -> 28.4 us
  starting transfers between devices: 17.7 us -> 37.7 us
    reduce_scatter x10 -> x6, waiting for transfers between devices: 435 us -> 70.8 us  [the longest x1 51.2 us: shards(): lax.psum_scatter(dot(attended, out_rows).astype(BF16), 'expert', scatter_...]
    all_to_all x4 -> x8, waiting for transfers between devices: 291 us -> 81.8 us  [the longest x7 81.8 us: exchange(): return lax.all_to_all(x, axes, split_axis=0, concat_axis=0, tiled=True)]
    all_gather x4 -> x0, blocking collectives: 163 us -> none  [the longest x1 122 us: shards(): lax.all_gather(router_weight, 'dp', axis=0, tiled=True)]
    all_to_all x0 -> x3, blocking collectives: none -> 151 us  [the longest x2 121 us: exchange(): return lax.all_to_all(x, axes, split_axis=0, concat_axis=0, tiled=True)]
    dot_general x60 -> x26, matrix products: 251 us -> 145 us  [the longest x25 143 us: dot(): return lax.dot_general(a, b, (dims, ((), ())), preferred_element_type=F32)]
    psum x1 -> x0, blocking collectives: 39.2 us -> none  [shards(): lax.psum((jnp.sum(attention_terms, axis=0), jnp.sum(mixture_terms, axis=0...]
    all_gather x8 -> x6, waiting for transfers between devices: 254 us -> 217 us  [the longest x2 70.4 us: dispatch(): gathered = lax.all_gather(rows, 'dp', axis=0, tiled=True)]
    reshape x8 -> x4, local copies, waits for them, and re-layouts: 39.7 us -> 8.44 us  [the longest x1 7.52 us: shards(): out_part.reshape(1, columns, width)]
  transfers between devices with their start and end apart: 24 -> 22, of which waited for: 20 -> 15; matrix products, arithmetic and copies ran while one was open for 19% -> 21% of each run, Pallas kernels for 0% -> 0%
where the time goes in v1:
time: 867 us; the launch traced here: 855 us
  waiting for transfers between devices  373 us (43%)
  blocking collectives  151 us (17%)
  matrix products  145 us (17%)
  local copies, waits for them, and re-layouts  58.6 us (7%)
  other arithmetic  45.7 us (5%)
  starting transfers between devices  37.7 us (4%)
  Pallas kernels  28.4 us (3%)
  between operations  15.9 us (2%)
    dot_general x25, matrix products, dot(): return lax.dot_general(a, b, (dims, ((), ())), preferred_element_type=F32)  143 us
    all_to_all x2, blocking collectives, exchange(): return lax.all_to_all(x, axes, split_axis=0, concat_axis=0, tiled=True)  121 us
    all_to_all x7, waiting for transfers between devices, exchange(): return lax.all_to_all(x, axes, split_axis=0, concat_axis=0, tiled=True)  81.8 us
    all_gather x2, waiting for transfers between devices, dispatch(): gathered = lax.all_gather(rows, 'dp', axis=0, tiled=True)  70.4 us
    all_gather x1, waiting for transfers between devices, shards(): lax.all_gather(jnp.concatenate([query_weight, key_matrix, value_matrix],...  51.3 us
    reduce_scatter x1, waiting for transfers between devices, shards(): lax.psum_scatter(dot(attended, out_rows).astype(BF16), 'expert', scatter_...  51.2 us
    all_gather x1, waiting for transfers between devices, shards(): out_rows = lax.all_gather(out_weight, 'dp', axis=0, tiled=True)  42.6 us
    all_gather x1, waiting for transfers between devices, shards(): lax.all_gather(after_grad.astype(BF16), 'expert', axis=0, tiled=True)  35.5 us
  transfers between devices with their start and end apart: 22, of which 15 were waited for; matrix products, arithmetic and copies ran while one was open for 21% of the time, Pallas kernels for 0%

profile of v1, /device:TPU:0, one launch (start us, length us, event | category | flops | bytes accessed | tf_op | source)
XLA Modules:
  0.0 855.3 jit_solution(14072775535073518677)
XLA Ops:
  10.1 2.0 pad_maximum_fusion.1
  13.4 2.0 fusion.28
  15.4 42.6 %all-gather.11.cloned.1.call-done = bf16[4096,256]{1,0:T(8,128)(2,1)} async-done(((bf16[1024,256]{1,0:T(8,128)(2,1)}), bf16[4096,256]{1,0:T(8,128)(2,1)}) %all-gather.11.cloned.1.call-update) | async-done | bytes 2097168 | tf_op jit(solution)/shard_map/all_gather | solution.py:305
  58.0 4.3 all-to-all-start
  62.4 51.3 %all-gather.9.cloned.1.call-done = bf16[2048,640]{1,0:T(8,128)(2,1)} async-done(((bf16[512,640]{1,0:T(8,128)(2,1)}), bf16[2048,640]{1,0:T(8,128)(2,1)}) %all-gather.9.cloned.1.call-update) | async-done | bytes 2621456 | tf_op jit(solution)/shard_map/all_gather | solution.py:287
  113.7 1.9 slice.97
  116.3 1.9 fusion.37
  123.9 6.6 concatenate.19
  130.4 4.0 copy.165
  134.4 17.2 %all-gather.7.cloned.1.call-done = bf16[1024,2048]{1,0:T(8,128)(2,1)} async-done(((bf16[128,2048]{1,0:T(8,128)(2,1)}), bf16[1024,2048]{1,0:T(8,128)(2,1)}) %all-gather.7.cloned.1.call-update) | async-done | bytes 4194320 | tf_op jit(solution)/shard_map/all_gather | solution.py:283
  151.6 6.2 fusion.55.q_ref.k_ref.v_ref
  157.9 12.7 %attend.1 = (bf16[1024,512]{1,0:T(8,128)(2,1)S(1)}, f32[4,1,1024]{2,1,0:T(1,128)S(1)}, bf16[1024,512]{1,0:T(8,128)(2,1)S(1)}) custom-call(s32[1]{0:T(128)S(6)} %copy.208.prefix_ref, f32[1024,768]{1,0:T(8,128)S(1)} %fusion.55.q_ref.k_ref.v_ref, f32[1024,768]{1,0:T(8,128)S(1)} %fusion.55.q_ref.k_ref.v_ref, f32[1024,768]{1,0:T(8,128)S(1)} %fusion.55.q_ref.k_ref.v_ref, ...), custom_call_target="tpu_custom_call" | custom-call | flops 1476395008 | bytes 6291456 | tf_op jit(solution)/shard_map/attend/pallas_call | solution.py:94
  172.5 4.4 convolution_convert_fusion.3
  177.0 51.2 %reduce-scatter.7.cloned.1.call-done = bf16[128,2048]{1,0:T(8,128)(2,1)} async-done(((bf16[1024,2048]{1,0:T(8,128)(2,1)}), bf16[128,2048]{1,0:T(8,128)(2,1)}) %reduce-scatter.7.cloned.1.call-update) | async-done | bytes 524304 | tf_op jit(solution)/shard_map/reduce_scatter | solution.py:369
  229.7 2.2 multiply_convert_fusion.8
  232.7 4.7 all-to-all-start.1
  237.5 13.8 %all-to-all-done.1 = bf16[32,32,128]{2,1,0:T(8,128)(2,1)} async-done(((bf16[32,32,128]{2,1,0:T(8,128)(2,1)}), bf16[32,32,128]{2,1,0:T(8,128)(2,1)}, u32[]{:S(2)}, u32[]{:S(2)}) %all-to-all-start.1) | async-done | bytes 262176 | tf_op jit(solution)/shard_map/all_to_all | solution.py:235
  252.0 5.6 all-to-all-start.3
  259.9 23.8 %all-gather.13.cloned.1.call-done = bf16[512,2048]{1,0:T(8,128)(2,1)} async-done(((bf16[128,2048]{1,0:T(8,128)(2,1)}), bf16[512,2048]{1,0:T(8,128)(2,1)}) %all-gather.13.cloned.1.call-update) | async-done | bytes 2097168 | tf_op jit(solution)/shard_map/all_gather | solution.py:349
  283.7 6.8 convolution_convert_fusion.2
  290.5 4.6 all-to-all-start.2
  295.8 46.6 %all-gather.15.cloned.1.call-done = bf16[512,2048]{1,0:T(8,128)(2,1)} async-done(((bf16[128,2048]{1,0:T(8,128)(2,1)}), bf16[512,2048]{1,0:T(8,128)(2,1)}) %all-gather.15.cloned.1.call-update) | async-done | bytes 2097168 | tf_op jit(solution)/shard_map/all_gather | solution.py:349
  342.3 6.8 convolution_convert_fusion
  349.1 3.6 all-to-all-done.2
  352.7 4.6 all-to-all-start.5
  360.4 4.0 fusion.53
  364.7 9.4 %fusion.13 = f32[1216,768]{1,0:T(8,128)} fusion(bf16[1216,2048]{1,0:T(8,128)(2,1)} %bitcast.21, bf16[1,2048,768]{2,1,0:T(8,128)(2,1)} %param.28), kind=kOutput, calls=%fused_computation.32 | convolution fusion | flops 3825205248 | bytes 11862016 | tf_op jit(solution)/shard_map/dot_general | solution.py:22
  374.1 8.3 fusion.9
  382.4 32.5 %all-to-all-done.5 = bf16[8,152,2048]{2,1,0:T(8,128)(2,1)} async-done(((bf16[8,152,2048]{2,1,0:T(8,128)(2,1)}), bf16[8,152,2048]{2,1,0:T(8,128)(2,1)}, u32[]{:S(2)}, u32[]{:S(2)}) %all-to-all-start.5) | async-done | bytes 4980768 | tf_op jit(solution)/shard_map/all_to_all | solution.py:235
  414.9 3.4 multiply_convert_fusion.1
  419.6 6.8 multiply_convert_fusion.5
  426.4 6.7 fusion.11
  433.0 6.8 add_convert_fusion
  439.9 60.0 %all_to_all.82 = bf16[8,152,2048]{2,1,0:T(8,128)(2,1)S(1)} all-to-all(bf16[8,152,2048]{2,1,0:T(8,128)(2,1)S(1)} %bitcast.172), channel_id=1, replica_groups=mesh['dp'=4,'expert'=8] {'expert'}, dimensions={0} | all-to-all | bytes 9961472 | tf_op jit(solution)/shard_map/all_to_all | solution.py:235
  499.8 4.2 bitcast_convert_fusion
  505.4 10.4 %fusion.1 = (f32[1216]{0:T(1024)S(1)}, f32[1216,2048]{1,0:T(8,128)}, bf16[1216,2048]{1,0:T(8,128)(2,1)}) fusion(bf16[1216,2048]{1,0:T(8,128)(2,1)} %bitcast.114, f32[1216]{0:T(1024)S(1)} %select_reduce_fusion, bf16[1216,768]{1,0:T(8,128)(2,1)} %get-tuple-element.148, bf16[1,768,2048]{2,1,0:T(8,128)(2,1)S(1)} %copy-done), kind=kOutput, calls=%fused_computation.3 | convolution fusion | flops 3842636544 | bytes 24946176 | tf_op jit(solution)/shard_map/dot_general | solution.py:22
  517.1 2.5 all-to-all-start.6
  519.7 7.3 all-to-all-done.6
  527.1 18.1 %reduce-scatter.11.cloned.1.call-done = bf16[128,2048]{1,0:T(8,128)(2,1)} async-done(((bf16[512,2048]{1,0:T(8,128)(2,1)}), bf16[128,2048]{1,0:T(8,128)(2,1)}) %reduce-scatter.11.cloned.1.call-update) | async-done | bytes 524304 | tf_op jit(solution)/shard_map/reduce_scatter | solution.py:358
  545.2 2.0 multiply_reduce_fusion.2
  548.9 35.5 %all-gather.17.cloned.1.call-done = bf16[1024,2048]{1,0:T(8,128)(2,1)} async-done(((bf16[128,2048]{1,0:T(8,128)(2,1)}), bf16[1024,2048]{1,0:T(8,128)(2,1)}) %all-gather.17.cloned.1.call-update) | async-done | bytes 4194320 | tf_op jit(solution)/shard_map/all_gather | solution.py:428
  584.4 5.2 convolution_convert_fusion.7.up_ref
  592.9 15.7 %attend_back.1 = (bf16[1024,512]{1,0:T(8,128)(2,1)S(1)}, bf16[1024,256]{1,0:T(8,128)(2,1)}, f32[1,128]{1,0:T(1,128)S(1)}, f32[1,128]{1,0:T(1,128)S(1)}) custom-call(s32[1]{0:T(128)S(6)} %copy.208.prefix_ref, f32[1024,768]{1,0:T(8,128)} %copy-done.2, f32[1024,768]{1,0:T(8,128)} %copy-done.2, f32[1024,768]{1,0:T(8,128)} %copy-done.2, ...), custom_call_target="tpu_custom_call" | custom-call | flops 3690987520 | bytes 7340032 | tf_op jit(solution)/shard_map/attend_back/pallas_call | solution.py:188
  614.3 5.1 convolution_convert_fusion.4
  619.6 4.6 fusion.15
  624.2 7.5 copy.175
  632.2 14.1 %reduce = bf16[2048,512]{1,0:T(8,128)(2,1)S(1)} reduce(bf16[2048,1,512]{2,1,0:T(2,128)(2,1)} %bitcast.165, bf16[]{:T(256)} %broadcast.167), dimensions={1}, to_apply=%bitcast.116.reduce_sub_computation | reduce | bytes 4194306
  646.3 3.8 reshape.206
  650.1 30.1 %all_to_all.83 = bf16[8,2,65536]{2,1,0:T(2,128)(2,1)S(1)} all-to-all(bf16[8,2,65536]{2,1,0:T(2,128)(2,1)} %reshape.206), channel_id=1, replica_groups=mesh['dp'=4,'expert'=8] {'expert'}, dimensions={0} | all-to-all | bytes 4194304 | tf_op jit(solution)/shard_map/all_to_all | solution.py:462
  680.2 4.3 reshape.207
  684.5 2.8 copy.185
  687.3 2.4 copy.176
  689.8 8.5 multiply_reduce_fusion
  698.4 61.3 %all_to_all.84 = bf16[8,152,2048]{2,1,0:T(8,128)(2,1)S(1)} all-to-all(bf16[8,152,2048]{2,1,0:T(8,128)(2,1)} %bitcast.169), channel_id=1, replica_groups=mesh['dp'=4,'expert'=8] {'expert'}, dimensions={0} | all-to-all | bytes 9961472 | tf_op jit(solution)/shard_map/all_to_all | solution.py:235
  759.7 4.2 bitcast_convert_fusion.1
  765.4 10.3 %fusion.4 = f32[1,768,2048]{2,1,0:T(8,128)} fusion(bf16[1216,768]{1,0:T(8,128)(2,1)S(1)} %copy-done.24, f32[1216,2048]{1,0:T(8,128)} %get-tuple-element.143, f32[1216]{0:T(1024)S(1)} %select_reduce_fusion), kind=kOutput, calls=%fused_computation.15 | convolution fusion | flops 3830185984 | bytes 18125568 | tf_op jit(solution)/shard_map/dot_general | solution.py:22
  776.8 3.8 all-to-all-start.9
  780.6 10.1 %convolution_bitcast_fusion.1 = f32[1,2048,768]{2,1,0:T(8,128)} fusion(bf16[1216,2048]{1,0:T(8,128)(2,1)} %bitcast.21, bf16[1216,768]{1,0:T(8,128)(2,1)} %copy-done.39), kind=kOutput, calls=%fused_computation.17 | convolution fusion | flops 3825205248 | bytes 13139968 | tf_op jit(solution)/shard_map/dot_general | solution.py:22
  791.6 6.1 all-to-all-start.10
  797.8 10.1 %convolution_bitcast_fusion = f32[1,2048,768]{2,1,0:T(8,128)} fusion(bf16[1216,2048]{1,0:T(8,128)(2,1)} %bitcast.21, bf16[1216,768]{1,0:T(8,128)(2,1)} %copy-done.40), kind=kOutput, calls=%fused_computation.16 | convolution fusion | flops 3825205248 | bytes 13139968 | tf_op jit(solution)/shard_map/dot_general | solution.py:22
  808.5 24.6 %all-to-all-done.10 = f32[32,34,128]{2,1,0:T(8,128)S(1)} async-done(((f32[32,34,128]{2,1,0:T(8,128)}), f32[32,34,128]{2,1,0:T(8,128)S(1)}, u32[]{:S(2)}, u32[]{:S(2)}) %all-to-all-start.10) | async-done | bytes 557088 | tf_op jit(solution)/shard_map/all_to_all | solution.py:235
  837.0 2.1 slice.108
  839.1 2.2 convert_element_type.204
  844.3 3.9 fusion.32
  (185 shorter events, 47.3 us)
Async XLA Ops:
  7.2 411.2 %copy-start = (bf16[1,768,2048]{2,1,0:T(8,128)(2,1)S(1)}, bf16[1,768,2048]{2,1,0:T(8,128)(2,1)}, u32[]{:S(2)}) copy-start(bf16[1,768,2048]{2,1,0:T(8,128)(2,1)} %param.30) | copy-start | bytes 9437188
  7.2 6.2 copy-start.27
  7.2 50.8 %all-gather.11.cloned.1.call-start = ((), (), s32[]{:S(2)}) async-start(), calls=%async_computation.19 | async-start | bytes 2621440 | tf_op jit(solution)/shard_map/all_gather | solution.py:305
  7.9 105.8 %all-gather.9.cloned.1.call-start = ((), (), s32[]{:S(2)}) async-start(), calls=%async_computation.18 | async-start | bytes 3276800 | tf_op jit(solution)/shard_map/all_gather | solution.py:287
  12.1 139.5 %all-gather.7.cloned.1.call-start = ((), (), s32[]{:S(2)}) async-start(), calls=%async_computation.17 | async-start | bytes 4718592 | tf_op jit(solution)/shard_map/all_gather | solution.py:283
  13.4 102.2 %copy-start.29 = (f32[128]{0:T(128)}, f32[128]{0:T(128)S(1)}, u32[]{:S(2)}) copy-start(f32[128]{0:T(128)S(1)} %add_rsqrt_fusion.2) | copy-start | bytes 1540
  58.0 72.4 %all-to-all-start = ((bf16[8,512,256]{2,1,0:T(8,128)(2,1)}), bf16[8,512,256]{2,1,0:T(8,128)(2,1)}, u32[]{:S(2)}, u32[]{:S(2)}) async-start(bf16[8,512,256]{2,1,0:T(8,128)(2,1)} %bitcast.179), calls=%async_computation | async-start | bytes 4194304 | tf_op jit(solution)/shard_map/all_to_all | solution.py:306
  62.3 165.9 %reduce-scatter.7.cloned.1.call-start = ((), (), s32[]{:S(2)}) async-start(), calls=%async_computation.20 | async-start | bytes 4718592 | tf_op jit(solution)/shard_map/reduce_scatter | solution.py:369
  115.6 5.5 collective-permute-start
  116.3 3.3 copy-start.22
  134.4 23.4 %copy-start.8 = (f32[128]{0:T(128)S(1)}, f32[128]{0:T(128)}, u32[]{:S(2)}) copy-start(f32[128]{0:T(128)} %param.27) | copy-start | bytes 1540
  134.4 23.4 %copy-start.9 = (f32[128]{0:T(128)S(1)}, f32[128]{0:T(128)}, u32[]{:S(2)}) copy-start(f32[128]{0:T(128)} %param.26) | copy-start | bytes 1540
  151.6 6.3 copy-start.4
  151.6 6.3 copy-start.6
  157.8 12.7 %copy-start.2 = (f32[1024,768]{1,0:T(8,128)}, f32[1024,768]{1,0:T(8,128)S(1)}, u32[]{:S(2)}) copy-start(f32[1024,768]{1,0:T(8,128)S(1)} %fusion.55.q_ref.k_ref.v_ref) | copy-start | bytes 9437188
  157.8 14.7 %copy-start.23 = (bf16[1,512,8,256]{1,3,2,0:T(8,128)(2,1)S(1)}, bf16[1,512,8,256]{1,3,2,0:T(8,128)(2,1)}, u32[]{:S(2)}) copy-start(bf16[1,512,8,256]{1,3,2,0:T(8,128)(2,1)} %copy.165) | copy-start | bytes 6291460
  170.6 1.0 copy-start.12
  171.5 1.0 copy-start.10
  176.9 52.8 %copy-start.26 = (f32[2048]{0:T(1024)S(1)}, f32[2048]{0:T(1024)}, u32[]{:S(2)}) copy-start(f32[2048]{0:T(1024)} %param.25) | copy-start | bytes 24580
  176.9 55.0 %copy-start.31 = (s32[128,8]{0,1:T(8,128)S(1)}, s32[128,8]{0,1:T(8,128)}, u32[]{:S(2)}) copy-start(s32[128,8]{0,1:T(8,128)} %param.17) | copy-start | bytes 12292
  176.9 74.4 %copy-start.32 = (bf16[512,4]{0,1:T(4,128)(2,1)S(1)}, bf16[512,4]{0,1:T(4,128)(2,1)}, u32[]{:S(2)}) copy-start(bf16[512,4]{0,1:T(4,128)(2,1)} %param.23) | copy-start | bytes 12292
  176.9 106.8 %all-gather.13.cloned.1.call-start = ((), (), s32[]{:S(2)}) async-start(), calls=%async_computation.21 | async-start | bytes 2621440 | tf_op jit(solution)/shard_map/all_gather | solution.py:349
  232.7 18.6 %all-to-all-start.1 = ((bf16[32,32,128]{2,1,0:T(8,128)(2,1)}), bf16[32,32,128]{2,1,0:T(8,128)(2,1)}, u32[]{:S(2)}, u32[]{:S(2)}) async-start(bf16[32,32,128]{2,1,0:T(8,128)(2,1)} %broadcast_in_dim.45), calls=%async_computation.2 | async-start | bytes 524288 | tf_op jit(solution)/shard_map/all_to_all | solution.py:235
  252.0 38.5 %all-to-all-start.3 = ((bf16[32,4,512]{2,1,0:T(4,128)(2,1)}), bf16[32,4,512]{2,1,0:T(4,128)(2,1)S(1)}, u32[]{:S(2)}, u32[]{:S(2)}) async-start(bf16[32,4,512]{2,1,0:T(4,128)(2,1)} %broadcast_in_dim.48), calls=%async_computation.4 | async-start | bytes 262144 | tf_op jit(solution)/shard_map/all_to_all | solution.py:235
  290.5 62.2 %all-to-all-start.2 = ((bf16[8,152,2048]{2,1,0:T(8,128)(2,1)}), bf16[8,152,2048]{2,1,0:T(8,128)(2,1)}, u32[]{:S(2)}, u32[]{:S(2)}) async-start(bf16[8,152,2048]{2,1,0:T(8,128)(2,1)} %bitcast.171), calls=%async_computation.3 | async-start | bytes 9961472 | tf_op jit(solution)/shard_map/all_to_all | solution.py:235
  295.2 47.1 %all-gather.15.cloned.1.call-start = ((), (), s32[]{:S(2)}) async-start(), calls=%async_computation.23 | async-start | bytes 2621440 | tf_op jit(solution)/shard_map/all_gather | solution.py:349
  352.7 62.2 %all-to-all-start.5 = ((bf16[8,152,2048]{2,1,0:T(8,128)(2,1)}), bf16[8,152,2048]{2,1,0:T(8,128)(2,1)}, u32[]{:S(2)}, u32[]{:S(2)}) async-start(bf16[8,152,2048]{2,1,0:T(8,128)(2,1)} %bitcast.170), calls=%async_computation.7 | async-start | bytes 9961472 | tf_op jit(solution)/shard_map/all_to_all | solution.py:235
  357.4 187.8 %reduce-scatter.11.cloned.1.call-start = ((), (), s32[]{:S(2)}) async-start(), calls=%async_computation.24 | async-start | bytes 2621440 | tf_op jit(solution)/shard_map/reduce_scatter | solution.py:358
  364.6 9.4 %copy-start.35 = (bf16[1,2048,768]{2,1,0:T(8,128)(2,1)S(1)}, bf16[1,2048,768]{2,1,0:T(8,128)(2,1)}, u32[]{:S(2)}) copy-start(bf16[1,2048,768]{2,1,0:T(8,128)(2,1)} %param.29) | copy-start | bytes 9437188
  414.9 3.5 copy-start.37
  414.9 4.7 copy-start.38
  419.6 6.8 copy-start.34
  426.4 6.7 copy-start.39
  426.4 6.7 copy-start.40
  426.4 6.7 copy-start.36
  515.8 31.4 %copy-start.17 = (bf16[128,2048]{1,0:T(8,128)(2,1)S(1)}, bf16[128,2048]{1,0:T(8,128)(2,1)}, u32[]{:S(2)}) copy-start(bf16[128,2048]{1,0:T(8,128)(2,1)} %param.16) | copy-start | bytes 1572868
  515.8 31.4 %copy-start.18 = (bf16[128,2048]{1,0:T(8,128)(2,1)S(1)}, bf16[128,2048]{1,0:T(8,128)(2,1)}, u32[]{:S(2)}) copy-start(bf16[128,2048]{1,0:T(8,128)(2,1)} %reduce-scatter.7.cloned.1.call-done) | copy-start | bytes 1572868
  515.8 31.4 %copy-start.21 = (bf16[128,2048]{1,0:T(8,128)(2,1)S(1)}, bf16[128,2048]{1,0:T(8,128)(2,1)}, u32[]{:S(2)}) copy-start(bf16[128,2048]{1,0:T(8,128)(2,1)} %param.31) | copy-start | bytes 1572868
  517.1 9.9 %all-to-all-start.6 = ((f32[32,1,128]{2,1,0:T(1,128)}), f32[32,1,128]{2,1,0:T(1,128)S(1)}, u32[]{:S(2)}, u32[]{:S(2)}) async-start(f32[32,1,128]{2,1,0:T(1,128)} %bitcast.35), calls=%async_computation.8 | async-start | bytes 32768 | tf_op jit(solution)/shard_map/all_to_all | solution.py:235
  519.6 64.8 %all-gather.17.cloned.1.call-start = ((), (), s32[]{:S(2)}) async-start(), calls=%async_computation.25 | async-start | bytes 4718592 | tf_op jit(solution)/shard_map/all_gather | solution.py:428
  547.2 42.5 %copy-start.19 = (f32[128,2048]{1,0:T(8,128)}, f32[128,2048]{1,0:T(8,128)S(1)}, u32[]{:S(2)}) copy-start(f32[128,2048]{1,0:T(8,128)S(1)} %get-tuple-element.173) | copy-start | bytes 3145732
  548.5 285.8 %reduce-scatter.15.cloned.1.call-start = ((), (), s32[]{:S(2)}) async-start(), calls=%async_computation.27 | async-start | bytes 3276800 | tf_op jit(solution)/shard_map/reduce_scatter | solution.py:458
  589.6 1.0 copy-start.5
  590.7 1.0 copy-start.7
  591.7 1.2 copy-start.13
  592.9 16.9 %copy-start.3 = (f32[1024,768]{1,0:T(8,128)S(1)}, f32[1024,768]{1,0:T(8,128)}, u32[]{:S(2)}) copy-start(f32[1024,768]{1,0:T(8,128)} %copy-done.2) | copy-start | bytes 9437188
  608.7 1.0 copy-start.14
  609.6 2.3 collective-permute-start.1
  610.1 4.1 copy-start.15
  610.1 4.1 copy-start.33
  614.2 5.1 copy-start.25
  614.3 5.4 copy-start.11
  619.4 219.7 %reduce-scatter.17.cloned.1.call-start = ((), (), s32[]{:S(2)}) async-start(), calls=%async_computation.28 | async-start | bytes 2621440 | tf_op jit(solution)/shard_map/reduce_scatter | solution.py:465
  687.3 2.5 copy-start.16
  689.7 151.6 %reduce-scatter.13.cloned.1.call-start = ((), (), s32[]{:S(2)}) async-start(), calls=%async_computation.26 | async-start | bytes 4718592 | tf_op jit(solution)/shard_map/reduce_scatter | solution.py:453
  698.3 146.0 %reduce-scatter.9.cloned.1.call-start = ((), (), s32[]{:S(2)}) async-start(), calls=%async_computation.22 | async-start | bytes 2621440 | tf_op jit(solution)/shard_map/reduce_scatter | solution.py:358
  763.9 1.5 copy-start.24
  765.4 10.3 %copy-start.20 = (bf16[128,2048]{1,0:T(8,128)(2,1)S(1)}, bf16[128,2048]{1,0:T(8,128)(2,1)}, u32[]{:S(2)}) copy-start(bf16[128,2048]{1,0:T(8,128)(2,1)} %multiply_convert_fusion.8) | copy-start | bytes 1572868
  776.8 13.9 %all-to-all-start.9 = ((bf16[32,4,512]{2,1,0:T(4,128)(2,1)}), bf16[32,4,512]{2,1,0:T(4,128)(2,1)S(1)}, u32[]{:S(2)}, u32[]{:S(2)}) async-start(bf16[32,4,512]{2,1,0:T(4,128)(2,1)} %copy.178), calls=%async_computation.15 | async-start | bytes 262144 | tf_op jit(solution)/shard_map/all_to_all | solution.py:235
  780.6 10.1 %copy-start.28 = (f32[2048]{0:T(1024)S(1)}, f32[2048]{0:T(1024)}, u32[]{:S(2)}) copy-start(f32[2048]{0:T(1024)} %param.24) | copy-start | bytes 24580
  791.6 41.5 %all-to-all-start.10 = ((f32[32,34,128]{2,1,0:T(8,128)}), f32[32,34,128]{2,1,0:T(8,128)S(1)}, u32[]{:S(2)}, u32[]{:S(2)}) async-start(f32[32,34,128]{2,1,0:T(8,128)} %broadcast_in_dim.52), calls=%async_computation.16 | async-start | bytes 1310720 | tf_op jit(solution)/shard_map/all_to_all | solution.py:235
  807.8 33.5 %copy-start.30 = (f32[128]{0:T(128)S(1)}, f32[128]{0:T(128)}, u32[]{:S(2)}) copy-start(f32[128]{0:T(128)} %copy-done.29) | copy-start | bytes 1540
  839.1 9.1 %copy-start.1 = (bf16[1,768,2048]{2,1,0:T(8,128)(2,1)S(1)}, bf16[1,768,2048]{2,1,0:T(8,128)(2,1)}, u32[]{:S(2)}) copy-start(bf16[1,768,2048]{2,1,0:T(8,128)(2,1)} %param.30) | copy-start | bytes 9437188
Sparse Core Ops, SparseCore 0:
  9.6 48.3 all-gather.10
  60.1 53.5 all-gather.8
  116.2 35.3 all-gather.6
  177.0 51.1 reduce-scatter.6
  232.0 51.6 all-gather.12
  297.3 45.0 all-gather.14
  504.1 41.0 reduce-scatter.10
  548.6 35.7 all-gather.16
  619.5 52.2 reduce-scatter.14
  689.9 42.7 reduce-scatter.16
  736.0 51.2 reduce-scatter.12
  789.4 54.8 reduce-scatter.8
